TPU v7x, 32 devices: a whole 2x2x4 slice. The times are simulated.
32 devices in a mesh: ja: 4 (over x, core), ka: 8 (over z, y).
Axes of the slice: x: 2, y: 2, z: 4, core: 2. Of those that a mesh axis runs over, the one named last changes fastest.
Arguments:
- blocks: bfloat16 [128, 128, 128, 128], P(('ja', 'ka')), may hold values from -6 to 6
- coords: int32 [128, 3], P(('ja', 'ka')), may hold values from 0 to 31, as said below
- live_counts: int32 [32], P(('ja', 'ka')), may hold values from 1 to 4, as said below
- mode2_factor: bfloat16 [4096, 512], P(('ja', 'ka')), may hold values from -0.52734375 to 0.52734375
- mode3_factor: bfloat16 [4096, 512], P(('ka', 'ja')), may hold values from -0.52734375 to 0.52734375
Outputs:
- mttkrp: float32 [512, 512], P(('ja', 'ka'))
Inputs may be any that keep to these rules, and one draw needn't show every extreme that they name: `coords`: column 0 lies in 0 to 3 and favours some popular row blocks. The device at index j of ja and k of ka holds slots whose column 1 lies in j * 8 to (j + 1) * 8 - 1 and whose column 2 lies in k * 4 to (k + 1) * 4 - 1. `live_counts`: slots of a device beyond its count are dead; some device in every draw has all 4 slots live.
All inputs are finite; a program needn't handle non-finite values.
Results may differ from a plain program's by a relative error of at most 0.0003.
Values may be sent and summed in bfloat16 or wider, within the bound.
No kernel may reach another device: no remote copies, remote signals or barrier semaphores. Data moves between devices by JAX's collectives and lax.ppermute only.
A program may use at most 64 MiB of HBM per device.

v0:
```python
import functools

import jax
import jax.numpy as jnp
from jax import lax
from jax.experimental import pallas as pl
from jax.experimental.pallas import tpu as pltpu
from jax.sharding import Mesh
from jax.sharding import PartitionSpec as P


IROWS_DEV = 16
CORES = 2
STEP_ROWS = 64
DOT_COLS = 256
PLACES = ("x", "core", "z", "y")
CHIPS = ("x", "z", "y")


def exchange(value, axis, code):
    size = lax.axis_size(axis)
    return lax.ppermute(value, axis, [(i, i ^ code) for i in range(size)])


def gather_pieces(own, far, near):
    far_size, near_size = lax.axis_size(far), lax.axis_size(near)
    pieces = {(0, 0): own}

    def fetch(code, source, axis, step):
        pieces[code] = exchange(pieces[source], axis, step)

    for far_code in range(far_size):
        low = far_code & -far_code
        rest = far_code ^ low
        if low and not rest:
            fetch((far_code, 0), (0, 0), far, far_code)
        elif low:
            fetch((far_code, 0), (rest, 0), far, low)
        for near_code in range(1, near_size):
            if rest:
                fetch((far_code, near_code), (low, near_code), far, rest)
            else:
                fetch((far_code, near_code), (far_code, 0), near, near_code)
    return [pieces[code] for code in sorted(pieces)]


def product_kernel(n_ja, n_ka, table, live, x_ref, *refs):
    mode2_refs, mode3_refs = refs[:n_ka], refs[n_ka : n_ka + n_ja]
    kept_ref, sent_ref, mode2, mode3 = refs[n_ka + n_ja :]
    slot, step, part_of = (pl.program_id(axis) for axis in range(3))
    rows, edge = x_ref.shape[1:3]

    @pl.when((slot == 0) & (step == 0) & (part_of == 0))
    def _():
        kept_ref[...] = jnp.zeros_like(kept_ref)
        sent_ref[...] = jnp.zeros_like(sent_ref)

    @pl.when(slot < live[0])
    def _():
        @pl.when((step == 0) & (part_of == 0))
        def _():
            for code, ref in enumerate(mode2_refs):

                @pl.when(table[slot, 1] == code)
                def _(ref=ref):
                    mode2[...] = ref[...].astype(jnp.float32)

            for code, ref in enumerate(mode3_refs):

                @pl.when(table[slot, 2] == code)
                def _(ref=ref):
                    mode3[...] = ref[...]

        cols = pl.ds(pl.multiple_of(part_of * DOT_COLS, DOT_COLS), DOT_COLS)
        cube = x_ref[0].reshape(rows * edge, edge)
        part = jnp.dot(cube, mode3[:, cols], preferred_element_type=jnp.float32)
        part = (part.reshape(rows, edge, DOT_COLS) * mode2[:, cols][None]).sum(axis=1)
        first = (table[slot, 0] * edge + step * rows) // IROWS_DEV
        column = first // n_ka
        chip = column // CORES * n_ka + first % n_ka

        def add_to(ref):
            for piece in range(rows // IROWS_DEV):
                ref[chip + piece, :, cols] += part[piece * IROWS_DEV : (piece + 1) * IROWS_DEV]

        pl.when(column % CORES == table[slot, 3])(functools.partial(add_to, kept_ref))
        pl.when(column % CORES != table[slot, 3])(functools.partial(add_to, sent_ref))


def products(blocks, table, live_counts, mode2_pieces, mode3_pieces):
    slots, edge = blocks.shape[:2]
    rank = mode2_pieces[0].shape[1]
    n_ka, n_ja = len(mode2_pieces), len(mode3_pieces)
    steps = edge // STEP_ROWS
    half_shape = (n_ja * n_ka // CORES, IROWS_DEV, rank)

    def block_at(slot, step, part_of, table, live):
        held = slot < live[0]
        return (
            jnp.where(held, slot, live[0] - 1),
            jnp.where(held, step, steps - 1),
            0,
            0,
        )

    half_spec = pl.BlockSpec(half_shape, lambda *_: (0, 0, 0))
    panel_spec = pl.BlockSpec((edge, rank), lambda *_: (0, 0))
    panels = mode2_pieces + mode3_pieces
    return pl.pallas_call(
        functools.partial(product_kernel, n_ja, n_ka),
        out_shape=[jax.ShapeDtypeStruct(half_shape, jnp.float32)] * 2,
        grid_spec=pltpu.PrefetchScalarGridSpec(
            num_scalar_prefetch=2,
            grid=(slots, steps, rank // DOT_COLS),
            in_specs=[pl.BlockSpec((1, STEP_ROWS, edge, edge), block_at)]
            + [panel_spec] * len(panels),
            out_specs=[half_spec] * 2,
            scratch_shapes=[
                pltpu.VMEM((edge, rank), jnp.float32),
                pltpu.VMEM((edge, rank), mode3_pieces[0].dtype),
            ],
        ),
        cost_estimate=pl.CostEstimate(
            flops=2 * slots * edge**3 * rank, bytes_accessed=2 * blocks.size, transcendentals=0
        ),
        compiler_params=pltpu.CompilerParams(vmem_limit_bytes=48 << 20),
    )(table, live_counts, blocks, *panels)


def on_device(blocks, coords, live_counts, mode2_factor, mode3_factor):
    x, core, z, y = (lax.axis_index(axis) for axis in PLACES)
    n_ja, n_ka = lax.axis_size(("x", "core")), lax.axis_size(("z", "y"))
    table = jnp.stack(
        [
            coords[:, 0],
            lax.rem(coords[:, 1], n_ka) ^ (z * lax.axis_size("y") + y),
            lax.rem(coords[:, 2], n_ja) ^ (x * CORES + core),
            jnp.broadcast_to(core, coords.shape[:1]),
        ],
        axis=1,
    )
    mode2_pieces = gather_pieces(mode2_factor, "z", "y")
    mode3_pieces = gather_pieces(mode3_factor, "x", "core")
    mode2_pieces[0] = pltpu.with_memory_space_constraint(mode2_factor, pltpu.HBM)
    mode3_pieces[0] = pltpu.with_memory_space_constraint(mode3_factor, pltpu.HBM)
    kept, sent = products(blocks, table, live_counts, mode2_pieces, mode3_pieces)
    received = exchange(sent, "core", 1)
    arrived = lax.all_to_all(kept + received, CHIPS, 0, 0, tiled=True)
    return arrived.sum(axis=0)


def solution(mesh):
    n_ja, n_ka = mesh.devices.shape
    near = 1
    while near * near * 4 <= n_ka:
        near *= 2
    places = Mesh(mesh.devices.reshape(n_ja // CORES, CORES, n_ka // near, near), PLACES)
    placed = (
        P(PLACES, None, None, None),
        P(PLACES, None),
        P(PLACES),
        P(PLACES, None),
        P(("z", "y", "x", "core"), None),
    )
    return jax.shard_map(
        on_device, mesh=places, in_specs=placed, out_specs=P(PLACES, None), check_vma=False
    )
```

profile of v0, /device:TPU:0, one launch (start us, length us, event | category | flops | bytes accessed | tf_op | source)
XLA Modules:
  0.0 73.9 jit_solution(1535028246350333272)
XLA Ops:
  0.0 3.1 %collective-permute-start.1 = (bf16[128,512]{1,0:T(8,128)(2,1)}, bf16[128,512]{1,0:T(8,128)(2,1)S(1)}, u32[]{:S(2)}, u32[]{:S(2)}) collective-permute-start(bf16[128,512]{1,0:T(8,128)(2,1)} %refs_0_.1), channel_id=1, source_target_pairs={{0,2},{2,0},{4,6},{6,4},{1,3},{3,1},{5,7},{7,5},{8,10},{10,8},{12,... | collective-permute-start | bytes 393224 | tf_op jit(solution)/shard_map/ppermute | solution.py:22
  3.1 0.0 collective-permute-start.7
  3.1 1.5 %collective-permute-start.8 = (bf16[128,512]{1,0:T(8,128)(2,1)}, bf16[128,512]{1,0:T(8,128)(2,1)S(1)}, u32[]{:S(2)}, u32[]{:S(2)}) collective-permute-start(bf16[128,512]{1,0:T(8,128)(2,1)} %refs_8_.1), channel_id=1, source_target_pairs={{0,16},{16,0},{1,17},{17,1},{2,18},{18,2},{3,19},{19,3},{4,20},{20... | collective-permute-start | bytes 393224 | tf_op jit(solution)/shard_map/ppermute | solution.py:22
  4.5 1.5 %collective-permute-start = (bf16[128,512]{1,0:T(8,128)(2,1)}, bf16[128,512]{1,0:T(8,128)(2,1)S(1)}, u32[]{:S(2)}, u32[]{:S(2)}) collective-permute-start(bf16[128,512]{1,0:T(8,128)(2,1)} %refs_0_.1), channel_id=1, source_target_pairs={{0,1},{1,0},{2,3},{3,2},{4,5},{5,4},{6,7},{7,6},{8,9},{9,8},{10,11... | collective-permute-start | bytes 393224 | tf_op jit(solution)/shard_map/ppermute | solution.py:22
  6.1 2.6 %collective-permute-start.3 = (bf16[128,512]{1,0:T(8,128)(2,1)}, bf16[128,512]{1,0:T(8,128)(2,1)S(1)}, u32[]{:S(2)}, u32[]{:S(2)}) collective-permute-start(bf16[128,512]{1,0:T(8,128)(2,1)} %refs_0_.1), channel_id=1, source_target_pairs={{0,4},{2,6},{4,0},{6,2},{1,5},{3,7},{5,1},{7,3},{8,12},{10,14},{12... | collective-permute-start | bytes 393224 | tf_op jit(solution)/shard_map/ppermute | solution.py:22
  9.3 0.1 pad.3.clone
  9.4 0.0 collective-permute-done.1.refs_2_
  9.4 0.5 collective-permute-start.2
  9.9 0.9 %fusion.4 = (s32[4,1]{1,0:T(4,128)S(1)}, s32[4,1]{1,0:T(4,128)S(1)}, s32[4,1]{1,0:T(4,128)S(1)}) fusion(s32[4,3]{1,0:T(4,128)} %param.6, s32[]{:T(128)S(6)} %add.10, s32[]{:T(128)S(6)} %add.9), kind=kLoop, calls=%fused_computation.9 | loop fusion | flops 56 | bytes 104 | tf_op jit(solution)/shard_map/slice | solution.py:135
  10.8 4.5 %collective-permute-done.3.refs_4_ = bf16[128,512]{1,0:T(8,128)(2,1)S(1)} collective-permute-done((bf16[128,512]{1,0:T(8,128)(2,1)}, bf16[128,512]{1,0:T(8,128)(2,1)S(1)}, u32[]{:S(2)}, u32[]{:S(2)}) %collective-permute-start.3) | collective-permute-done | bytes 131104 | tf_op jit(solution)/shard_map/ppermute | solution.py:22
  15.2 0.0 collective-permute-start.5
  15.2 0.0 collective-permute-done.7.refs_9_
  15.2 0.6 collective-permute-start.4
  15.8 0.0 collective-permute-done.8.refs_10_
  15.8 0.0 collective-permute-start.9
  15.8 0.0 collective-permute-done.2.refs_3_
  15.8 3.1 %collective-permute-start.6 = (bf16[128,512]{1,0:T(8,128)(2,1)S(1)}, bf16[128,512]{1,0:T(8,128)(2,1)S(1)}, u32[]{:S(2)}, u32[]{:S(2)}) collective-permute-start(bf16[128,512]{1,0:T(8,128)(2,1)S(1)} %collective-permute-done.2.refs_3_), channel_id=1, source_target_pairs={{0,4},{2,6},{4,0},{6,2},{1,5},{3,7},{5,1},{7,3},{8,12},{10,14},{12... | collective-permute-start | bytes 393224 | tf_op jit(solution)/shard_map/ppermute | solution.py:22
  19.0 0.1 add_add_fusion.table
  19.0 0.0 collective-permute-done.refs_1_
  19.0 0.0 collective-permute-done.9.refs_11_
  19.0 2.7 %collective-permute-done.5.refs_6_ = bf16[128,512]{1,0:T(8,128)(2,1)S(1)} collective-permute-done((bf16[128,512]{1,0:T(8,128)(2,1)S(1)}, bf16[128,512]{1,0:T(8,128)(2,1)S(1)}, u32[]{:S(2)}, u32[]{:S(2)}) %collective-permute-start.5) | collective-permute-done | bytes 131104 | tf_op jit(solution)/shard_map/ppermute | solution.py:22
  21.7 0.0 collective-permute-done.4.refs_5_
  21.7 4.2 %collective-permute-done.6.refs_7_ = bf16[128,512]{1,0:T(8,128)(2,1)S(1)} collective-permute-done((bf16[128,512]{1,0:T(8,128)(2,1)S(1)}, bf16[128,512]{1,0:T(8,128)(2,1)S(1)}, u32[]{:S(2)}, u32[]{:S(2)}) %collective-permute-start.6) | collective-permute-done | bytes 131104 | tf_op jit(solution)/shard_map/ppermute | solution.py:22
  25.9 8.5 %shard_map.55 = (f32[16,16,512]{2,1,0:T(8,128)S(1)}, f32[16,16,512]{2,1,0:T(8,128)S(1)}) custom-call(s32[4,4]{1,0:T(4,128)S(1)} %add_add_fusion.table, s32[1]{0:T(128)S(6)} %copy.6.live, bf16[4,128,128,128]{3,2,1,0:T(8,128)(2,1)} %x_ref.1, bf16[128,512]{1,0:T(8,128)(2,1)} %refs_0_.1, bf16[128,512]{1,0:T(8,128)(2,1)S(1)} %collective-permute-done.refs_1_, ...), custom_call_target="tpu_custom_call" | custom-call | flops 8589934592 | bytes 16777216 | tf_op jit(solution)/shard_map/pallas_call | solution.py:109
  34.5 5.6 %collective-permute-start.10 = (f32[16,16,512]{2,1,0:T(8,128)S(1)}, f32[16,16,512]{2,1,0:T(8,128)S(1)}, u32[]{:S(2)}, u32[]{:S(2)}) collective-permute-start(f32[16,16,512]{2,1,0:T(8,128)S(1)} %get-tuple-element.8), channel_id=1, source_target_pairs={{0,8},{8,0},{1,9},{9,1},{2,10},{10,2},{3,11},{11,3},{4,12},{12,4},... | collective-permute-start | bytes 1572872 | tf_op jit(solution)/shard_map/ppermute | solution.py:22
  40.1 1.5 %collective-permute-done.10 = f32[16,16,512]{2,1,0:T(8,128)S(1)} collective-permute-done((f32[16,16,512]{2,1,0:T(8,128)S(1)}, f32[16,16,512]{2,1,0:T(8,128)S(1)}, u32[]{:S(2)}, u32[]{:S(2)}) %collective-permute-start.10) | collective-permute-done | bytes 524320 | tf_op jit(solution)/shard_map/ppermute | solution.py:22
  41.6 0.1 add.11
  41.7 31.6 %all_to_all.5 = f32[16,16,512]{2,1,0:T(8,128)S(1)} all-to-all(f32[16,16,512]{2,1,0:T(8,128)S(1)} %add.11), channel_id=1, replica_groups=mesh['x'=2,'core'=2,'z'=4,'y'=2] {'x','z','y'}, dimensions={0} | all-to-all | bytes 1048576 | tf_op jit(solution)/shard_map/all_to_all | solution.py:148
  73.2 0.6 reduce_sum.9
Async XLA Ops:
  0.0 9.4 %collective-permute-start.1 = (bf16[128,512]{1,0:T(8,128)(2,1)}, bf16[128,512]{1,0:T(8,128)(2,1)S(1)}, u32[]{:S(2)}, u32[]{:S(2)}) collective-permute-start(bf16[128,512]{1,0:T(8,128)(2,1)} %refs_0_.1), channel_id=1, source_target_pairs={{0,2},{2,0},{4,6},{6,4},{1,3},{3,1},{5,7},{7,5},{8,10},{10,8},{12,... | collective-permute-start | bytes 393224 | tf_op jit(solution)/shard_map/ppermute | solution.py:22
  3.1 12.2 %collective-permute-start.7 = (bf16[128,512]{1,0:T(8,128)(2,1)}, bf16[128,512]{1,0:T(8,128)(2,1)S(1)}, u32[]{:S(2)}, u32[]{:S(2)}) collective-permute-start(bf16[128,512]{1,0:T(8,128)(2,1)} %refs_8_.1), channel_id=1, source_target_pairs={{0,8},{8,0},{1,9},{9,1},{2,10},{10,2},{3,11},{11,3},{4,12},{12,4},... | collective-permute-start | bytes 393224 | tf_op jit(solution)/shard_map/ppermute | solution.py:22
  3.1 12.8 %collective-permute-start.8 = (bf16[128,512]{1,0:T(8,128)(2,1)}, bf16[128,512]{1,0:T(8,128)(2,1)S(1)}, u32[]{:S(2)}, u32[]{:S(2)}) collective-permute-start(bf16[128,512]{1,0:T(8,128)(2,1)} %refs_8_.1), channel_id=1, source_target_pairs={{0,16},{16,0},{1,17},{17,1},{2,18},{18,2},{3,19},{19,3},{4,20},{20... | collective-permute-start | bytes 393224 | tf_op jit(solution)/shard_map/ppermute | solution.py:22
  4.5 14.5 %collective-permute-start = (bf16[128,512]{1,0:T(8,128)(2,1)}, bf16[128,512]{1,0:T(8,128)(2,1)S(1)}, u32[]{:S(2)}, u32[]{:S(2)}) collective-permute-start(bf16[128,512]{1,0:T(8,128)(2,1)} %refs_0_.1), channel_id=1, source_target_pairs={{0,1},{1,0},{2,3},{3,2},{4,5},{5,4},{6,7},{7,6},{8,9},{9,8},{10,11... | collective-permute-start | bytes 393224 | tf_op jit(solution)/shard_map/ppermute | solution.py:22
  6.1 9.2 %collective-permute-start.3 = (bf16[128,512]{1,0:T(8,128)(2,1)}, bf16[128,512]{1,0:T(8,128)(2,1)S(1)}, u32[]{:S(2)}, u32[]{:S(2)}) collective-permute-start(bf16[128,512]{1,0:T(8,128)(2,1)} %refs_0_.1), channel_id=1, source_target_pairs={{0,4},{2,6},{4,0},{6,2},{1,5},{3,7},{5,1},{7,3},{8,12},{10,14},{12... | collective-permute-start | bytes 393224 | tf_op jit(solution)/shard_map/ppermute | solution.py:22
  9.4 6.4 %collective-permute-start.2 = (bf16[128,512]{1,0:T(8,128)(2,1)S(1)}, bf16[128,512]{1,0:T(8,128)(2,1)S(1)}, u32[]{:S(2)}, u32[]{:S(2)}) collective-permute-start(bf16[128,512]{1,0:T(8,128)(2,1)S(1)} %collective-permute-done.1.refs_2_), channel_id=1, source_target_pairs={{0,1},{1,0},{2,3},{3,2},{4,5},{5,4},{6,7},{7,6},{8,9},{9,8},{10,11... | collective-permute-start | bytes 393224 | tf_op jit(solution)/shard_map/ppermute | solution.py:22
  15.2 6.5 %collective-permute-start.5 = (bf16[128,512]{1,0:T(8,128)(2,1)S(1)}, bf16[128,512]{1,0:T(8,128)(2,1)S(1)}, u32[]{:S(2)}, u32[]{:S(2)}) collective-permute-start(bf16[128,512]{1,0:T(8,128)(2,1)S(1)} %collective-permute-done.3.refs_4_), channel_id=1, source_target_pairs={{0,2},{2,0},{4,6},{6,4},{1,3},{3,1},{5,7},{7,5},{8,10},{10,8},{12,... | collective-permute-start | bytes 393224 | tf_op jit(solution)/shard_map/ppermute | solution.py:22
  15.2 6.5 %collective-permute-start.4 = (bf16[128,512]{1,0:T(8,128)(2,1)S(1)}, bf16[128,512]{1,0:T(8,128)(2,1)S(1)}, u32[]{:S(2)}, u32[]{:S(2)}) collective-permute-start(bf16[128,512]{1,0:T(8,128)(2,1)S(1)} %collective-permute-done.3.refs_4_), channel_id=1, source_target_pairs={{0,1},{1,0},{2,3},{3,2},{4,5},{5,4},{6,7},{7,6},{8,9},{9,8},{10,11... | collective-permute-start | bytes 393224 | tf_op jit(solution)/shard_map/ppermute | solution.py:22
  15.8 3.2 %collective-permute-start.9 = (bf16[128,512]{1,0:T(8,128)(2,1)S(1)}, bf16[128,512]{1,0:T(8,128)(2,1)S(1)}, u32[]{:S(2)}, u32[]{:S(2)}) collective-permute-start(bf16[128,512]{1,0:T(8,128)(2,1)S(1)} %collective-permute-done.8.refs_10_), channel_id=1, source_target_pairs={{0,8},{8,0},{1,9},{9,1},{2,10},{10,2},{3,11},{11,3},{4,12},{12,4},... | collective-permute-start | bytes 393224 | tf_op jit(solution)/shard_map/ppermute | solution.py:22
  15.8 10.1 %collective-permute-start.6 = (bf16[128,512]{1,0:T(8,128)(2,1)S(1)}, bf16[128,512]{1,0:T(8,128)(2,1)S(1)}, u32[]{:S(2)}, u32[]{:S(2)}) collective-permute-start(bf16[128,512]{1,0:T(8,128)(2,1)S(1)} %collective-permute-done.2.refs_3_), channel_id=1, source_target_pairs={{0,4},{2,6},{4,0},{6,2},{1,5},{3,7},{5,1},{7,3},{8,12},{10,14},{12... | collective-permute-start | bytes 393224 | tf_op jit(solution)/shard_map/ppermute | solution.py:22
  34.5 7.1 %collective-permute-start.10 = (f32[16,16,512]{2,1,0:T(8,128)S(1)}, f32[16,16,512]{2,1,0:T(8,128)S(1)}, u32[]{:S(2)}, u32[]{:S(2)}) collective-permute-start(f32[16,16,512]{2,1,0:T(8,128)S(1)} %get-tuple-element.8), channel_id=1, source_target_pairs={{0,8},{8,0},{1,9},{9,1},{2,10},{10,2},{3,11},{11,3},{4,12},{12,4},... | collective-permute-start | bytes 1572872 | tf_op jit(solution)/shard_map/ppermute | solution.py:22
where the time goes:
time: 74.3 us; the launch traced here: 73.9 us
  blocking collectives  31.6 us (43%)
  starting transfers between devices  18.5 us (25%)
  waiting for transfers between devices  12.9 us (17%)
  Pallas kernels  8.52 us (11%)
  other arithmetic  1.67 us (2%)
    all_to_all x1, blocking collectives, on_device(): arrived = lax.all_to_all(kept + received, CHIPS, 0, 0, tiled=True)  31.6 us
    ppermute x11, starting transfers between devices, exchange(): return lax.ppermute(value, axis, [(i, i ^ code) for i in range(size)])  18.5 us
    ppermute x11, waiting for transfers between devices, exchange(): return lax.ppermute(value, axis, [(i, i ^ code) for i in range(size)])  12.9 us
    pallas_call x1, Pallas kernels, products(): pl.pallas_call(functools.partial(product_kernel, n_ja, n_ka), out_shape=[...  8.52 us
  transfers between devices with their start and end apart: 11, of which 4 were waited for; matrix products, arithmetic and copies ran while one was open for 1% of the time, Pallas kernels for 0%

commit v1 on v0

--- a/solution.py
+++ b/solution.py
@@ -12,7 +12,7 @@
 IROWS_DEV = 16
 CORES = 2
 STEP_ROWS = 64
-DOT_COLS = 256
+DOT_COLS = 512
 PLACES = ("x", "core", "z", "y")
 CHIPS = ("x", "z", "y")
 
@@ -46,14 +46,9 @@
 
 def product_kernel(n_ja, n_ka, table, live, x_ref, *refs):
     mode2_refs, mode3_refs = refs[:n_ka], refs[n_ka : n_ka + n_ja]
-    kept_ref, sent_ref, mode2, mode3 = refs[n_ka + n_ja :]
+    kept_ref, sent_ref, mode2, mode3 = refs[n_ka + n_ja + 2 :]
     slot, step, part_of = (pl.program_id(axis) for axis in range(3))
     rows, edge = x_ref.shape[1:3]
-
-    @pl.when((slot == 0) & (step == 0) & (part_of == 0))
-    def _():
-        kept_ref[...] = jnp.zeros_like(kept_ref)
-        sent_ref[...] = jnp.zeros_like(sent_ref)
 
     @pl.when(slot < live[0])
     def _():
@@ -103,9 +98,10 @@
             0,
         )
 
-    half_spec = pl.BlockSpec(half_shape, lambda *_: (0, 0, 0))
-    panel_spec = pl.BlockSpec((edge, rank), lambda *_: (0, 0))
+    in_place = pl.BlockSpec(memory_space=pltpu.VMEM)
+    own_spec = pl.BlockSpec((edge, rank), lambda *_: (0, 0))
     panels = mode2_pieces + mode3_pieces
+    empty = jnp.zeros(half_shape, jnp.float32)
     return pl.pallas_call(
         functools.partial(product_kernel, n_ja, n_ka),
         out_shape=[jax.ShapeDtypeStruct(half_shape, jnp.float32)] * 2,
@@ -113,8 +109,10 @@
             num_scalar_prefetch=2,
             grid=(slots, steps, rank // DOT_COLS),
             in_specs=[pl.BlockSpec((1, STEP_ROWS, edge, edge), block_at)]
-            + [panel_spec] * len(panels),
-            out_specs=[half_spec] * 2,
+            + ([own_spec] + [in_place] * (n_ka - 1))
+            + ([own_spec] + [in_place] * (n_ja - 1))
+            + [in_place] * 2,
+            out_specs=[in_place] * 2,
             scratch_shapes=[
                 pltpu.VMEM((edge, rank), jnp.float32),
                 pltpu.VMEM((edge, rank), mode3_pieces[0].dtype),
@@ -123,8 +121,9 @@
         cost_estimate=pl.CostEstimate(
             flops=2 * slots * edge**3 * rank, bytes_accessed=2 * blocks.size, transcendentals=0
         ),
+        input_output_aliases={3 + len(panels): 0, 4 + len(panels): 1},
         compiler_params=pltpu.CompilerParams(vmem_limit_bytes=48 << 20),
-    )(table, live_counts, blocks, *panels)
+    )(table, live_counts, blocks, *panels, empty, empty + 0)
 
 
 def on_device(blocks, coords, live_counts, mode2_factor, mode3_factor):

time: 74.3 us -> 68.5 us (0.922)
  waiting for transfers between devices: 12.9 us -> 11 us
  blocking collectives: 31.6 us -> 30 us
  starting transfers between devices: 18.5 us -> 17.3 us
  Pallas kernels: 8.52 us -> 7.42 us
    ppermute x11, waiting for transfers between devices: 12.9 us -> 11 us  [exchange(): return lax.ppermute(value, axis, [(i, i ^ code) for i in range(size)])]
    all_to_all x1, blocking collectives: 31.6 us -> 30 us  [on_device(): arrived = lax.all_to_all(kept + received, CHIPS, 0, 0, tiled=True)]
    ppermute x11, starting transfers between devices: 18.5 us -> 17.3 us  [exchange(): return lax.ppermute(value, axis, [(i, i ^ code) for i in range(size)])]
    pallas_call x1, Pallas kernels: 8.52 us -> 7.42 us  [products(): pl.pallas_call(functools.partial(product_kernel, n_ja, n_ka), out_shape=[...]
  transfers between devices with their start and end apart: 11 -> 11, of which waited for: 4 -> 6; matrix products, arithmetic and copies ran while one was open for 1% -> 1% of each run, Pallas kernels for 0% -> 0%
where the time goes in v1:
time: 68.5 us; the launch traced here: 68.3 us
  blocking collectives  30 us (44%)
  starting transfers between devices  17.3 us (25%)
  waiting for transfers between devices  11 us (16%)
  Pallas kernels  7.42 us (11%)
  other arithmetic  1.67 us (2%)
  between operations  0.69 us (1%)
    all_to_all x1, blocking collectives, on_device(): arrived = lax.all_to_all(kept + received, CHIPS, 0, 0, tiled=True)  30 us
    ppermute x11, starting transfers between devices, exchange(): return lax.ppermute(value, axis, [(i, i ^ code) for i in range(size)])  17.3 us
    ppermute x11, waiting for transfers between devices, exchange(): return lax.ppermute(value, axis, [(i, i ^ code) for i in range(size)])  11 us
    pallas_call x1, Pallas kernels, products(): pl.pallas_call(functools.partial(product_kernel, n_ja, n_ka), out_shape=[...  7.42 us
  transfers between devices with their start and end apart: 11, of which 6 were waited for; matrix products, arithmetic and copies ran while one was open for 1% of the time, Pallas kernels for 0%

profile of v1, /device:TPU:0, one launch (start us, length us, event | category | flops | bytes accessed | tf_op | source)
XLA Modules:
  0.0 68.3 jit_solution(10248485975386028421)
XLA Ops:
  0.0 3.1 %collective-permute-start.1 = (bf16[128,512]{1,0:T(8,128)(2,1)}, bf16[128,512]{1,0:T(8,128)(2,1)S(1)}, u32[]{:S(2)}, u32[]{:S(2)}) collective-permute-start(bf16[128,512]{1,0:T(8,128)(2,1)} %refs_0_.1), channel_id=1, source_target_pairs={{0,2},{2,0},{4,6},{6,4},{1,3},{3,1},{5,7},{7,5},{8,10},{10,8},{12,... | collective-permute-start | bytes 393224 | tf_op jit(solution)/shard_map/ppermute | solution.py:22
  3.1 2.6 %collective-permute-start.3 = (bf16[128,512]{1,0:T(8,128)(2,1)}, bf16[128,512]{1,0:T(8,128)(2,1)S(1)}, u32[]{:S(2)}, u32[]{:S(2)}) collective-permute-start(bf16[128,512]{1,0:T(8,128)(2,1)} %refs_0_.1), channel_id=1, source_target_pairs={{0,4},{2,6},{4,0},{6,2},{1,5},{3,7},{5,1},{7,3},{8,12},{10,14},{12... | collective-permute-start | bytes 393224 | tf_op jit(solution)/shard_map/ppermute | solution.py:22
  5.6 1.5 %collective-permute-start = (bf16[128,512]{1,0:T(8,128)(2,1)}, bf16[128,512]{1,0:T(8,128)(2,1)S(1)}, u32[]{:S(2)}, u32[]{:S(2)}) collective-permute-start(bf16[128,512]{1,0:T(8,128)(2,1)} %refs_0_.1), channel_id=1, source_target_pairs={{0,1},{1,0},{2,3},{3,2},{4,5},{5,4},{6,7},{7,6},{8,9},{9,8},{10,11... | collective-permute-start | bytes 393224 | tf_op jit(solution)/shard_map/ppermute | solution.py:22
  7.2 1.5 %collective-permute-start.8 = (bf16[128,512]{1,0:T(8,128)(2,1)}, bf16[128,512]{1,0:T(8,128)(2,1)S(1)}, u32[]{:S(2)}, u32[]{:S(2)}) collective-permute-start(bf16[128,512]{1,0:T(8,128)(2,1)} %refs_8_.1), channel_id=1, source_target_pairs={{0,16},{16,0},{1,17},{17,1},{2,18},{18,2},{3,19},{19,3},{4,20},{20... | collective-permute-start | bytes 393224 | tf_op jit(solution)/shard_map/ppermute | solution.py:22
  8.7 0.0 collective-permute-start.7
  9.3 0.1 pad.3.clone
  9.4 0.0 collective-permute-done.1.refs_2_
  9.4 1.0 %collective-permute-start.2 = (bf16[128,512]{1,0:T(8,128)(2,1)S(1)}, bf16[128,512]{1,0:T(8,128)(2,1)S(1)}, u32[]{:S(2)}, u32[]{:S(2)}) collective-permute-start(bf16[128,512]{1,0:T(8,128)(2,1)S(1)} %collective-permute-done.1.refs_2_), channel_id=1, source_target_pairs={{0,1},{1,0},{2,3},{3,2},{4,5},{5,4},{6,7},{7,6},{8,9},{9,8},{10,11... | collective-permute-start | bytes 393224 | tf_op jit(solution)/shard_map/ppermute | solution.py:22
  10.4 0.9 %fusion.4 = (s32[4,1]{1,0:T(4,128)S(1)}, s32[4,1]{1,0:T(4,128)S(1)}, s32[4,1]{1,0:T(4,128)S(1)}) fusion(s32[4,3]{1,0:T(4,128)} %param.6, s32[]{:T(128)S(6)} %add.10, s32[]{:T(128)S(6)} %add.9), kind=kLoop, calls=%fused_computation.9 | loop fusion | flops 56 | bytes 104 | tf_op jit(solution)/shard_map/slice | solution.py:134
  11.3 0.7 %collective-permute-done.3.refs_4_ = bf16[128,512]{1,0:T(8,128)(2,1)S(1)} collective-permute-done((bf16[128,512]{1,0:T(8,128)(2,1)}, bf16[128,512]{1,0:T(8,128)(2,1)S(1)}, u32[]{:S(2)}, u32[]{:S(2)}) %collective-permute-start.3) | collective-permute-done | bytes 131104 | tf_op jit(solution)/shard_map/ppermute | solution.py:22
  12.0 1.5 %collective-permute-start.4 = (bf16[128,512]{1,0:T(8,128)(2,1)S(1)}, bf16[128,512]{1,0:T(8,128)(2,1)S(1)}, u32[]{:S(2)}, u32[]{:S(2)}) collective-permute-start(bf16[128,512]{1,0:T(8,128)(2,1)S(1)} %collective-permute-done.3.refs_4_), channel_id=1, source_target_pairs={{0,1},{1,0},{2,3},{3,2},{4,5},{5,4},{6,7},{7,6},{8,9},{9,8},{10,11... | collective-permute-start | bytes 393224 | tf_op jit(solution)/shard_map/ppermute | solution.py:22
  13.5 0.0 collective-permute-done.8.refs_10_
  13.5 0.4 collective-permute-start.5
  13.9 0.0 collective-permute-done.refs_1_
  14.0 0.0 collective-permute-start.9
  14.0 1.8 %collective-permute-done.2.refs_3_ = bf16[128,512]{1,0:T(8,128)(2,1)S(1)} collective-permute-done((bf16[128,512]{1,0:T(8,128)(2,1)S(1)}, bf16[128,512]{1,0:T(8,128)(2,1)S(1)}, u32[]{:S(2)}, u32[]{:S(2)}) %collective-permute-start.2) | collective-permute-done | bytes 131104 | tf_op jit(solution)/shard_map/ppermute | solution.py:22
  15.8 1.2 %collective-permute-start.6 = (bf16[128,512]{1,0:T(8,128)(2,1)S(1)}, bf16[128,512]{1,0:T(8,128)(2,1)S(1)}, u32[]{:S(2)}, u32[]{:S(2)}) collective-permute-start(bf16[128,512]{1,0:T(8,128)(2,1)S(1)} %collective-permute-done.2.refs_3_), channel_id=1, source_target_pairs={{0,4},{2,6},{4,0},{6,2},{1,5},{3,7},{5,1},{7,3},{8,12},{10,14},{12... | collective-permute-start | bytes 393224 | tf_op jit(solution)/shard_map/ppermute | solution.py:22
  17.0 0.1 add_add_fusion.table
  17.1 0.0 collective-permute-done.7.refs_9_
  17.1 1.0 %collective-permute-done.4.refs_5_ = bf16[128,512]{1,0:T(8,128)(2,1)S(1)} collective-permute-done((bf16[128,512]{1,0:T(8,128)(2,1)S(1)}, bf16[128,512]{1,0:T(8,128)(2,1)S(1)}, u32[]{:S(2)}, u32[]{:S(2)}) %collective-permute-start.4) | collective-permute-done | bytes 131104 | tf_op jit(solution)/shard_map/ppermute | solution.py:22
  18.1 0.4 collective-permute-done.5.refs_6_
  18.5 0.0 collective-permute-done.9.refs_11_
  18.5 5.6 %collective-permute-done.6.refs_7_ = bf16[128,512]{1,0:T(8,128)(2,1)S(1)} collective-permute-done((bf16[128,512]{1,0:T(8,128)(2,1)S(1)}, bf16[128,512]{1,0:T(8,128)(2,1)S(1)}, u32[]{:S(2)}, u32[]{:S(2)}) %collective-permute-start.6) | collective-permute-done | bytes 131104 | tf_op jit(solution)/shard_map/ppermute | solution.py:22
  24.1 0.1 broadcast_in_dim.3.clone.refs_13_
  24.2 7.4 %shard_map.55 = (f32[16,16,512]{2,1,0:T(8,128)S(1)}, f32[16,16,512]{2,1,0:T(8,128)S(1)}) custom-call(s32[4,4]{1,0:T(4,128)S(1)} %add_add_fusion.table, s32[1]{0:T(128)S(6)} %copy.11.live, bf16[4,128,128,128]{3,2,1,0:T(8,128)(2,1)} %x_ref.1, bf16[128,512]{1,0:T(8,128)(2,1)} %refs_0_.1, ...), custom_call_target="tpu_custom_call", output_to_operand_aliasing={{0}: (15, {}), {1}: (16, {})} | custom-call | flops 8589934592 | bytes 16777216 | tf_op jit(solution)/shard_map/pallas_call | solution.py:105
  31.6 4.4 %collective-permute-start.10 = (f32[16,16,512]{2,1,0:T(8,128)S(1)}, f32[16,16,512]{2,1,0:T(8,128)S(1)}, u32[]{:S(2)}, u32[]{:S(2)}) collective-permute-start(f32[16,16,512]{2,1,0:T(8,128)S(1)} %get-tuple-element.8), channel_id=1, source_target_pairs={{0,8},{8,0},{1,9},{9,1},{2,10},{10,2},{3,11},{11,3},{4,12},{12,4},... | collective-permute-start | bytes 1572872 | tf_op jit(solution)/shard_map/ppermute | solution.py:22
  36.0 1.5 %collective-permute-done.10 = f32[16,16,512]{2,1,0:T(8,128)S(1)} collective-permute-done((f32[16,16,512]{2,1,0:T(8,128)S(1)}, f32[16,16,512]{2,1,0:T(8,128)S(1)}, u32[]{:S(2)}, u32[]{:S(2)}) %collective-permute-start.10) | collective-permute-done | bytes 524320 | tf_op jit(solution)/shard_map/ppermute | solution.py:22
  37.6 0.1 add.11
  37.7 30.0 %all_to_all.5 = f32[16,16,512]{2,1,0:T(8,128)S(1)} all-to-all(f32[16,16,512]{2,1,0:T(8,128)S(1)} %add.11), channel_id=1, replica_groups=mesh['x'=2,'core'=2,'z'=4,'y'=2] {'x','z','y'}, dimensions={0} | all-to-all | bytes 1048576 | tf_op jit(solution)/shard_map/all_to_all | solution.py:147
  67.7 0.6 reduce_sum.9
  (1 shorter events, 0.0 us)
Async XLA Ops:
  0.0 9.4 %collective-permute-start.1 = (bf16[128,512]{1,0:T(8,128)(2,1)}, bf16[128,512]{1,0:T(8,128)(2,1)S(1)}, u32[]{:S(2)}, u32[]{:S(2)}) collective-permute-start(bf16[128,512]{1,0:T(8,128)(2,1)} %refs_0_.1), channel_id=1, source_target_pairs={{0,2},{2,0},{4,6},{6,4},{1,3},{3,1},{5,7},{7,5},{8,10},{10,8},{12,... | collective-permute-start | bytes 393224 | tf_op jit(solution)/shard_map/ppermute | solution.py:22
  3.1 8.9 %collective-permute-start.3 = (bf16[128,512]{1,0:T(8,128)(2,1)}, bf16[128,512]{1,0:T(8,128)(2,1)S(1)}, u32[]{:S(2)}, u32[]{:S(2)}) collective-permute-start(bf16[128,512]{1,0:T(8,128)(2,1)} %refs_0_.1), channel_id=1, source_target_pairs={{0,4},{2,6},{4,0},{6,2},{1,5},{3,7},{5,1},{7,3},{8,12},{10,14},{12... | collective-permute-start | bytes 393224 | tf_op jit(solution)/shard_map/ppermute | solution.py:22
  5.6 8.3 %collective-permute-start = (bf16[128,512]{1,0:T(8,128)(2,1)}, bf16[128,512]{1,0:T(8,128)(2,1)S(1)}, u32[]{:S(2)}, u32[]{:S(2)}) collective-permute-start(bf16[128,512]{1,0:T(8,128)(2,1)} %refs_0_.1), channel_id=1, source_target_pairs={{0,1},{1,0},{2,3},{3,2},{4,5},{5,4},{6,7},{7,6},{8,9},{9,8},{10,11... | collective-permute-start | bytes 393224 | tf_op jit(solution)/shard_map/ppermute | solution.py:22
  7.2 6.4 %collective-permute-start.8 = (bf16[128,512]{1,0:T(8,128)(2,1)}, bf16[128,512]{1,0:T(8,128)(2,1)S(1)}, u32[]{:S(2)}, u32[]{:S(2)}) collective-permute-start(bf16[128,512]{1,0:T(8,128)(2,1)} %refs_8_.1), channel_id=1, source_target_pairs={{0,16},{16,0},{1,17},{17,1},{2,18},{18,2},{3,19},{19,3},{4,20},{20... | collective-permute-start | bytes 393224 | tf_op jit(solution)/shard_map/ppermute | solution.py:22
  8.7 8.4 %collective-permute-start.7 = (bf16[128,512]{1,0:T(8,128)(2,1)}, bf16[128,512]{1,0:T(8,128)(2,1)S(1)}, u32[]{:S(2)}, u32[]{:S(2)}) collective-permute-start(bf16[128,512]{1,0:T(8,128)(2,1)} %refs_8_.1), channel_id=1, source_target_pairs={{0,8},{8,0},{1,9},{9,1},{2,10},{10,2},{3,11},{11,3},{4,12},{12,4},... | collective-permute-start | bytes 393224 | tf_op jit(solution)/shard_map/ppermute | solution.py:22
  9.4 6.4 %collective-permute-start.2 = (bf16[128,512]{1,0:T(8,128)(2,1)S(1)}, bf16[128,512]{1,0:T(8,128)(2,1)S(1)}, u32[]{:S(2)}, u32[]{:S(2)}) collective-permute-start(bf16[128,512]{1,0:T(8,128)(2,1)S(1)} %collective-permute-done.1.refs_2_), channel_id=1, source_target_pairs={{0,1},{1,0},{2,3},{3,2},{4,5},{5,4},{6,7},{7,6},{8,9},{9,8},{10,11... | collective-permute-start | bytes 393224 | tf_op jit(solution)/shard_map/ppermute | solution.py:22
  12.0 6.1 %collective-permute-start.4 = (bf16[128,512]{1,0:T(8,128)(2,1)S(1)}, bf16[128,512]{1,0:T(8,128)(2,1)S(1)}, u32[]{:S(2)}, u32[]{:S(2)}) collective-permute-start(bf16[128,512]{1,0:T(8,128)(2,1)S(1)} %collective-permute-done.3.refs_4_), channel_id=1, source_target_pairs={{0,1},{1,0},{2,3},{3,2},{4,5},{5,4},{6,7},{7,6},{8,9},{9,8},{10,11... | collective-permute-start | bytes 393224 | tf_op jit(solution)/shard_map/ppermute | solution.py:22
  13.5 5.0 %collective-permute-start.5 = (bf16[128,512]{1,0:T(8,128)(2,1)S(1)}, bf16[128,512]{1,0:T(8,128)(2,1)S(1)}, u32[]{:S(2)}, u32[]{:S(2)}) collective-permute-start(bf16[128,512]{1,0:T(8,128)(2,1)S(1)} %collective-permute-done.3.refs_4_), channel_id=1, source_target_pairs={{0,2},{2,0},{4,6},{6,4},{1,3},{3,1},{5,7},{7,5},{8,10},{10,8},{12,... | collective-permute-start | bytes 393224 | tf_op jit(solution)/shard_map/ppermute | solution.py:22
  14.0 4.5 %collective-permute-start.9 = (bf16[128,512]{1,0:T(8,128)(2,1)S(1)}, bf16[128,512]{1,0:T(8,128)(2,1)S(1)}, u32[]{:S(2)}, u32[]{:S(2)}) collective-permute-start(bf16[128,512]{1,0:T(8,128)(2,1)S(1)} %collective-permute-done.8.refs_10_), channel_id=1, source_target_pairs={{0,8},{8,0},{1,9},{9,1},{2,10},{10,2},{3,11},{11,3},{4,12},{12,4},... | collective-permute-start | bytes 393224 | tf_op jit(solution)/shard_map/ppermute | solution.py:22
  15.8 8.3 %collective-permute-start.6 = (bf16[128,512]{1,0:T(8,128)(2,1)S(1)}, bf16[128,512]{1,0:T(8,128)(2,1)S(1)}, u32[]{:S(2)}, u32[]{:S(2)}) collective-permute-start(bf16[128,512]{1,0:T(8,128)(2,1)S(1)} %collective-permute-done.2.refs_3_), channel_id=1, source_target_pairs={{0,4},{2,6},{4,0},{6,2},{1,5},{3,7},{5,1},{7,3},{8,12},{10,14},{12... | collective-permute-start | bytes 393224 | tf_op jit(solution)/shard_map/ppermute | solution.py:22
  31.6 6.0 %collective-permute-start.10 = (f32[16,16,512]{2,1,0:T(8,128)S(1)}, f32[16,16,512]{2,1,0:T(8,128)S(1)}, u32[]{:S(2)}, u32[]{:S(2)}) collective-permute-start(f32[16,16,512]{2,1,0:T(8,128)S(1)} %get-tuple-element.8), channel_id=1, source_target_pairs={{0,8},{8,0},{1,9},{9,1},{2,10},{10,2},{3,11},{11,3},{4,12},{12,4},... | collective-permute-start | bytes 1572872 | tf_op jit(solution)/shard_map/ppermute | solution.py:22

commit v2 on v1

v2 whole, which is shorter than its diff:
```python
import functools

import jax
import jax.numpy as jnp
from jax import lax
from jax.experimental import pallas as pl
from jax.experimental.pallas import tpu as pltpu
from jax.sharding import Mesh
from jax.sharding import PartitionSpec as P


IROWS_DEV = 16
CORES = 2
STEP_ROWS = 64
PLACES = ("x", "core", "z", "y")
CHIPS = ("x", "z", "y")


def exchange(value, axis, code):
    size = lax.axis_size(axis)
    return lax.ppermute(value, axis, [(i, i ^ code) for i in range(size)])


def gather_pieces(own, far, near):
    far_size, near_size = lax.axis_size(far), lax.axis_size(near)
    pieces = {(0, 0): own}

    def fetch(code, source, axis, step):
        pieces[code] = exchange(pieces[source], axis, step)

    for far_code in range(far_size):
        low = far_code & -far_code
        rest = far_code ^ low
        if low and not rest:
            fetch((far_code, 0), (0, 0), far, far_code)
        elif low:
            fetch((far_code, 0), (rest, 0), far, low)
        for near_code in range(1, near_size):
            if rest:
                fetch((far_code, near_code), (low, near_code), far, rest)
            else:
                fetch((far_code, near_code), (far_code, 0), near, near_code)
    return [pieces[code] for code in sorted(pieces)]


def block_of(blocks_ref, index, steps):
    rows = pl.ds(index % steps * STEP_ROWS, STEP_ROWS)
    return blocks_ref.at[index // steps, rows]


def fetch_kernel(blocks_ref, mode2_ref, mode3_ref, *refs):
    cubes_ref, own2_ref, own3_ref, kept_ref, sent_ref, sems = refs
    copies = [
        pltpu.make_async_copy(source, target, sems.at[order])
        for order, (source, target) in enumerate(
            (
                (block_of(blocks_ref, 0, 1), cubes_ref.at[0]),
                (mode2_ref, own2_ref),
                (mode3_ref, own3_ref),
            )
        )
    ]
    for copy in copies:
        copy.start()
    kept_ref[...] = jnp.zeros_like(kept_ref)
    sent_ref[...] = jnp.zeros_like(sent_ref)
    for copy in copies:
        copy.wait()


def fetch_local(blocks, mode2_own, mode3_own, half_shape):
    edge = blocks.shape[1]
    in_hbm = pl.BlockSpec(memory_space=pl.ANY)
    in_place = pl.BlockSpec(memory_space=pltpu.VMEM)
    return pl.pallas_call(
        fetch_kernel,
        out_shape=[
            jax.ShapeDtypeStruct((2, STEP_ROWS, edge, edge), blocks.dtype),
            jax.ShapeDtypeStruct(mode2_own.shape, mode2_own.dtype),
            jax.ShapeDtypeStruct(mode3_own.shape, mode3_own.dtype),
            jax.ShapeDtypeStruct(half_shape, jnp.float32),
            jax.ShapeDtypeStruct(half_shape, jnp.float32),
        ],
        in_specs=[in_hbm] * 3,
        out_specs=[in_place] * 5,
        scratch_shapes=[pltpu.SemaphoreType.DMA((3,))],
        cost_estimate=pl.CostEstimate(flops=0, bytes_accessed=4 << 20, transcendentals=0),
        compiler_params=pltpu.CompilerParams(vmem_limit_bytes=2 << 20),
    )(blocks, mode2_own, mode3_own)


def product_kernel(n_ja, n_ka, steps, table, live, blocks_ref, *refs):
    mode2_refs, mode3_refs = refs[:n_ka], refs[n_ka : n_ka + n_ja]
    cubes_ref, kept_ref, sent_ref, mode2, mode3, sems = refs[n_ka + n_ja + 3 :]
    index = pl.program_id(0)
    slot, step = index // steps, index % steps
    edge, rank = mode2.shape
    last = live[0] * steps - 1

    def cubes_copy(at):
        side = at % 2
        return pltpu.make_async_copy(
            block_of(blocks_ref, at, steps), cubes_ref.at[side], sems.at[side]
        )

    @pl.when(index < last)
    def _():
        cubes_copy(index + 1).start()

    @pl.when(index <= last)
    def _():
        @pl.when(step == 0)
        def _():
            for code, ref in enumerate(mode2_refs):

                @pl.when(table[slot, 1] == code)
                def _(ref=ref):
                    mode2[...] = ref[...].astype(jnp.float32)

            for code, ref in enumerate(mode3_refs):

                @pl.when(table[slot, 2] == code)
                def _(ref=ref):
                    mode3[...] = ref[...]

        @pl.when(index > 0)
        def _():
            cubes_copy(index).wait()

        cube = cubes_ref[index % 2].reshape(STEP_ROWS * edge, edge)
        part = jnp.dot(cube, mode3[...], preferred_element_type=jnp.float32)
        part = (part.reshape(STEP_ROWS, edge, rank) * mode2[...][None]).sum(axis=1)
        first = (table[slot, 0] * edge + step * STEP_ROWS) // IROWS_DEV
        column = first // n_ka
        chip = column // CORES * n_ka + first % n_ka

        def add_to(ref):
            for piece in range(STEP_ROWS // IROWS_DEV):
                ref[chip + piece] += part[piece * IROWS_DEV : (piece + 1) * IROWS_DEV]

        pl.when(column % CORES == table[slot, 3])(functools.partial(add_to, kept_ref))
        pl.when(column % CORES != table[slot, 3])(functools.partial(add_to, sent_ref))


def products(blocks, table, live_counts, mode2_pieces, mode3_pieces, buffers):
    slots, edge = blocks.shape[:2]
    rank = mode2_pieces[0].shape[1]
    n_ka, n_ja = len(mode2_pieces), len(mode3_pieces)
    steps = edge // STEP_ROWS
    in_hbm = pl.BlockSpec(memory_space=pl.ANY)
    in_place = pl.BlockSpec(memory_space=pltpu.VMEM)
    panels = mode2_pieces + mode3_pieces
    _, kept, sent = pl.pallas_call(
        functools.partial(product_kernel, n_ja, n_ka, steps),
        out_shape=[jax.ShapeDtypeStruct(buffer.shape, buffer.dtype) for buffer in buffers],
        grid_spec=pltpu.PrefetchScalarGridSpec(
            num_scalar_prefetch=2,
            grid=(slots * steps,),
            in_specs=[in_hbm] + [in_place] * (len(panels) + len(buffers)),
            out_specs=[in_place] * len(buffers),
            scratch_shapes=[
                pltpu.VMEM((edge, rank), jnp.float32),
                pltpu.VMEM((edge, rank), mode3_pieces[0].dtype),
                pltpu.SemaphoreType.DMA((2,)),
            ],
        ),
        cost_estimate=pl.CostEstimate(
            flops=2 * slots * edge**3 * rank, bytes_accessed=2 * blocks.size, transcendentals=0
        ),
        input_output_aliases={3 + len(panels) + order: order for order in range(len(buffers))},
        compiler_params=pltpu.CompilerParams(vmem_limit_bytes=40 << 20),
    )(table, live_counts, blocks, *panels, *buffers)
    return kept, sent


def on_device(blocks, coords, live_counts, mode2_factor, mode3_factor):
    x, core, z, y = (lax.axis_index(axis) for axis in PLACES)
    n_ja, n_ka = lax.axis_size(("x", "core")), lax.axis_size(("z", "y"))
    table = jnp.stack(
        [
            coords[:, 0],
            lax.rem(coords[:, 1], n_ka) ^ (z * lax.axis_size("y") + y),
            lax.rem(coords[:, 2], n_ja) ^ (x * CORES + core),
            jnp.broadcast_to(core, coords.shape[:1]),
        ],
        axis=1,
    )
    mode2_pieces = gather_pieces(mode2_factor, "z", "y")
    mode3_pieces = gather_pieces(mode3_factor, "x", "core")
    blocks = pltpu.with_memory_space_constraint(blocks, pltpu.HBM)
    half_shape = (n_ja * n_ka // CORES, IROWS_DEV, mode2_factor.shape[1])
    cubes, mode2_pieces[0], mode3_pieces[0], kept, sent = fetch_local(
        blocks,
        pltpu.with_memory_space_constraint(mode2_factor, pltpu.HBM),
        pltpu.with_memory_space_constraint(mode3_factor, pltpu.HBM),
        half_shape,
    )
    kept, sent = products(
        blocks, table, live_counts, mode2_pieces, mode3_pieces, (cubes, kept, sent)
    )
    received = exchange(sent, "core", 1)
    arrived = lax.all_to_all(kept + received, CHIPS, 0, 0, tiled=True)
    return arrived.sum(axis=0)


def solution(mesh):
    n_ja, n_ka = mesh.devices.shape
    near = 1
    while near * near * 4 <= n_ka:
        near *= 2
    places = Mesh(mesh.devices.reshape(n_ja // CORES, CORES, n_ka // near, near), PLACES)
    placed = (
        P(PLACES, None, None, None),
        P(PLACES, None),
        P(PLACES),
        P(PLACES, None),
        P(("z", "y", "x", "core"), None),
    )
    return jax.shard_map(
        on_device, mesh=places, in_specs=placed, out_specs=P(PLACES, None), check_vma=False
    )
```

time: 68.5 us -> 71.5 us (1.044)
  local copies, waits for them, and re-layouts: 0.18 us -> 4.21 us
  starting transfers between devices: 17.3 us -> 14.8 us
  waiting for transfers between devices: 11 us -> 13.1 us
  other arithmetic: 1.67 us -> 0.89 us
    unnamed x0 -> x6, local copies, waits for them, and re-layouts: none -> 4.13 us
    ppermute x11, starting transfers between devices: 17.3 us -> 14.8 us  [exchange(): return lax.ppermute(value, axis, [(i, i ^ code) for i in range(size)])]
    ppermute x11, waiting for transfers between devices: 11 us -> 13.1 us  [exchange(): return lax.ppermute(value, axis, [(i, i ^ code) for i in range(size)])]
    slice x1, other arithmetic: 0.87 us -> 0.08 us  [on_device(): coords[:, 0]]
    pallas_call x1 -> x2, Pallas kernels: 7.42 us -> 7.39 us  [the longest x1 5.76 us: products(): pl.pallas_call(functools.partial(product_kernel, n_ja, n_ka, steps), out_...]
  transfers between devices with their start and end apart: 11 -> 11, of which waited for: 6 -> 6; matrix products, arithmetic and copies ran while one was open for 1% -> 0% of each run, Pallas kernels for 0% -> 2%
where the time goes in v2:
time: 71.5 us; the launch traced here: 71.3 us
  blocking collectives  30.2 us (42%)
  starting transfers between devices  14.8 us (21%)
  waiting for transfers between devices  13.1 us (18%)
  Pallas kernels  7.39 us (10%)
  local copies, waits for them, and re-layouts  4.21 us (6%)
  other arithmetic  0.89 us (1%)
    all_to_all x1, blocking collectives, on_device(): arrived = lax.all_to_all(kept + received, CHIPS, 0, 0, tiled=True)  30.2 us
    ppermute x11, starting transfers between devices, exchange(): return lax.ppermute(value, axis, [(i, i ^ code) for i in range(size)])  14.8 us
    ppermute x11, waiting for transfers between devices, exchange(): return lax.ppermute(value, axis, [(i, i ^ code) for i in range(size)])  13.1 us
    pallas_call x1, Pallas kernels, products(): pl.pallas_call(functools.partial(product_kernel, n_ja, n_ka, steps), out_...  5.76 us
    unnamed x6, local copies, waits for them, and re-layouts  4.13 us
    pallas_call x1, Pallas kernels, fetch_local(): pl.pallas_call(fetch_kernel, out_shape=[jax.ShapeDtypeStruct((2, STEP_ROW...  1.63 us
  transfers between devices with their start and end apart: 11, of which 6 were waited for; matrix products, arithmetic and copies ran while one was open for 0% of the time, Pallas kernels for 2%

profile of v2, /device:TPU:0, one launch (start us, length us, event | category | flops | bytes accessed | tf_op | source)
XLA Modules:
  0.0 71.3 jit_solution(3293308750687014676)
XLA Ops:
  0.0 3.1 %collective-permute-start.1 = (bf16[128,512]{1,0:T(8,128)(2,1)}, bf16[128,512]{1,0:T(8,128)(2,1)S(1)}, u32[]{:S(2)}, u32[]{:S(2)}) collective-permute-start(bf16[128,512]{1,0:T(8,128)(2,1)} %mode2_ref.1), channel_id=1, source_target_pairs={{0,2},{2,0},{4,6},{6,4},{1,3},{3,1},{5,7},{7,5},{8,10},{10,8},{12,... | collective-permute-start | bytes 393224 | tf_op jit(solution)/shard_map/ppermute | solution.py:21
  3.1 1.5 %collective-permute-start.8 = (bf16[128,512]{1,0:T(8,128)(2,1)}, bf16[128,512]{1,0:T(8,128)(2,1)S(1)}, u32[]{:S(2)}, u32[]{:S(2)}) collective-permute-start(bf16[128,512]{1,0:T(8,128)(2,1)} %mode3_ref.1), channel_id=1, source_target_pairs={{0,16},{16,0},{1,17},{17,1},{2,18},{18,2},{3,19},{19,3},{4,20},{20... | collective-permute-start | bytes 393224 | tf_op jit(solution)/shard_map/ppermute | solution.py:21
  4.5 0.0 collective-permute-start.7
  4.5 1.5 %collective-permute-start = (bf16[128,512]{1,0:T(8,128)(2,1)}, bf16[128,512]{1,0:T(8,128)(2,1)S(1)}, u32[]{:S(2)}, u32[]{:S(2)}) collective-permute-start(bf16[128,512]{1,0:T(8,128)(2,1)} %mode2_ref.1), channel_id=1, source_target_pairs={{0,1},{1,0},{2,3},{3,2},{4,5},{5,4},{6,7},{7,6},{8,9},{9,8},{10,11... | collective-permute-start | bytes 393224 | tf_op jit(solution)/shard_map/ppermute | solution.py:21
  6.1 2.6 %collective-permute-start.3 = (bf16[128,512]{1,0:T(8,128)(2,1)}, bf16[128,512]{1,0:T(8,128)(2,1)S(1)}, u32[]{:S(2)}, u32[]{:S(2)}) collective-permute-start(bf16[128,512]{1,0:T(8,128)(2,1)} %mode2_ref.1), channel_id=1, source_target_pairs={{0,4},{2,6},{4,0},{6,2},{1,5},{3,7},{5,1},{7,3},{8,12},{10,14},{12... | collective-permute-start | bytes 393224 | tf_op jit(solution)/shard_map/ppermute | solution.py:21
  9.3 0.0 copy-start.2
  9.3 1.6 %shard_map.55 = (bf16[2,64,128,128]{3,2,1,0:T(8,128)(2,1)S(1)}, bf16[128,512]{1,0:T(8,128)(2,1)S(1)}, bf16[128,512]{1,0:T(8,128)(2,1)S(1)}, f32[16,16,512]{2,1,0:T(8,128)S(1)}, f32[16,16,512]{2,1,0:T(8,128)S(1)}) custom-call(bf16[4,128,128,128]{3,2,1,0:T(8,128)(2,1)} %blocks_ref.3, bf16[128,512]{1,0:T(8,128)(2,1)} %mode2_ref.1, bf16[128,512]{1,0:T(8,128)(2,1)} %mode3_ref.1), custom_call_target="tpu_custom_call" | custom-call | bytes 4194304 | tf_op jit(solution)/shard_map/pallas_call | solution.py:75
  11.0 0.0 copy-start
  11.0 1.9 %copy-done = bf16[2,64,128,128]{3,2,1,0:T(8,128)(2,1)} copy-done((bf16[2,64,128,128]{3,2,1,0:T(8,128)(2,1)}, bf16[2,64,128,128]{3,2,1,0:T(8,128)(2,1)S(1)}, u32[]{:S(2)}) %copy-start) | copy-done | bytes 4194328
  12.9 0.1 pad.3.clone
  13.0 0.0 collective-permute-done.1.refs_2_
  13.0 0.5 collective-permute-start.2
  13.5 0.0 copy-done.2
  13.5 0.1 fusion.4
  13.6 2.0 %collective-permute-done.3.refs_4_ = bf16[128,512]{1,0:T(8,128)(2,1)S(1)} collective-permute-done((bf16[128,512]{1,0:T(8,128)(2,1)}, bf16[128,512]{1,0:T(8,128)(2,1)S(1)}, u32[]{:S(2)}, u32[]{:S(2)}) %collective-permute-start.3) | collective-permute-done | bytes 131104 | tf_op jit(solution)/shard_map/ppermute | solution.py:21
  15.5 0.0 collective-permute-start.5
  15.5 0.0 collective-permute-done.8.refs_10_
  15.5 0.6 collective-permute-start.4
  16.1 0.0 collective-permute-done.7.refs_9_
  16.1 0.0 collective-permute-start.9
  16.1 2.4 %collective-permute-done.2.refs_3_ = bf16[128,512]{1,0:T(8,128)(2,1)S(1)} collective-permute-done((bf16[128,512]{1,0:T(8,128)(2,1)S(1)}, bf16[128,512]{1,0:T(8,128)(2,1)S(1)}, u32[]{:S(2)}, u32[]{:S(2)}) %collective-permute-start.2) | collective-permute-done | bytes 131104 | tf_op jit(solution)/shard_map/ppermute | solution.py:21
  18.5 0.8 %collective-permute-start.6 = (bf16[128,512]{1,0:T(8,128)(2,1)S(1)}, bf16[128,512]{1,0:T(8,128)(2,1)S(1)}, u32[]{:S(2)}, u32[]{:S(2)}) collective-permute-start(bf16[128,512]{1,0:T(8,128)(2,1)S(1)} %collective-permute-done.2.refs_3_), channel_id=1, source_target_pairs={{0,4},{2,6},{4,0},{6,2},{1,5},{3,7},{5,1},{7,3},{8,12},{10,14},{12... | collective-permute-start | bytes 393224 | tf_op jit(solution)/shard_map/ppermute | solution.py:21
  19.2 0.1 add_add_fusion.table
  19.3 0.0 collective-permute-done.refs_1_
  19.3 0.0 collective-permute-done.9.refs_11_
  19.3 1.7 %collective-permute-done.5.refs_6_ = bf16[128,512]{1,0:T(8,128)(2,1)S(1)} collective-permute-done((bf16[128,512]{1,0:T(8,128)(2,1)S(1)}, bf16[128,512]{1,0:T(8,128)(2,1)S(1)}, u32[]{:S(2)}, u32[]{:S(2)}) %collective-permute-start.5) | collective-permute-done | bytes 131104 | tf_op jit(solution)/shard_map/ppermute | solution.py:21
  21.0 0.2 collective-permute-done.4.refs_5_
  21.1 5.4 %collective-permute-done.6.refs_7_ = bf16[128,512]{1,0:T(8,128)(2,1)S(1)} collective-permute-done((bf16[128,512]{1,0:T(8,128)(2,1)S(1)}, bf16[128,512]{1,0:T(8,128)(2,1)S(1)}, u32[]{:S(2)}, u32[]{:S(2)}) %collective-permute-start.6) | collective-permute-done | bytes 131104 | tf_op jit(solution)/shard_map/ppermute | solution.py:21
  26.5 0.0 copy-start.1
  26.5 2.2 %copy-done.1 = bf16[2,64,128,128]{3,2,1,0:T(8,128)(2,1)S(1)} copy-done((bf16[2,64,128,128]{3,2,1,0:T(8,128)(2,1)S(1)}, bf16[2,64,128,128]{3,2,1,0:T(8,128)(2,1)}, u32[]{:S(2)}) %copy-start.1) | copy-done | bytes 4194328
  28.7 5.8 %shard_map.56 = (bf16[2,64,128,128]{3,2,1,0:T(8,128)(2,1)S(1)}, f32[16,16,512]{2,1,0:T(8,128)S(1)}, f32[16,16,512]{2,1,0:T(8,128)S(1)}) custom-call(s32[4,4]{1,0:T(4,128)S(1)} %add_add_fusion.table, s32[1]{0:T(128)S(6)} %copy.12.live, bf16[4,128,128,128]{3,2,1,0:T(8,128)(2,1)} %blocks_ref.3, ...), custom_call_target="tpu_custom_call", output_to_operand_aliasing={{0}: (15, {}), {1}: (16, {}), {2}: (17, {})} | custom-call | flops 8589934592 | bytes 16777216 | tf_op jit(solution)/shard_map/pallas_call | solution.py:153
  34.5 4.3 %collective-permute-start.10 = (f32[16,16,512]{2,1,0:T(8,128)S(1)}, f32[16,16,512]{2,1,0:T(8,128)S(1)}, u32[]{:S(2)}, u32[]{:S(2)}) collective-permute-start(f32[16,16,512]{2,1,0:T(8,128)S(1)} %get-tuple-element.18), channel_id=1, source_target_pairs={{0,8},{8,0},{1,9},{9,1},{2,10},{10,2},{3,11},{11,3},{4,12},{12,4},... | collective-permute-start | bytes 1572872 | tf_op jit(solution)/shard_map/ppermute | solution.py:21
  38.8 1.5 %collective-permute-done.10 = f32[16,16,512]{2,1,0:T(8,128)S(1)} collective-permute-done((f32[16,16,512]{2,1,0:T(8,128)S(1)}, f32[16,16,512]{2,1,0:T(8,128)S(1)}, u32[]{:S(2)}, u32[]{:S(2)}) %collective-permute-start.10) | collective-permute-done | bytes 524320 | tf_op jit(solution)/shard_map/ppermute | solution.py:21
  40.4 0.1 add.11
  40.5 30.2 %all_to_all.5 = f32[16,16,512]{2,1,0:T(8,128)S(1)} all-to-all(f32[16,16,512]{2,1,0:T(8,128)S(1)} %add.11), channel_id=1, replica_groups=mesh['x'=2,'core'=2,'z'=4,'y'=2] {'x','z','y'}, dimensions={0} | all-to-all | bytes 1048576 | tf_op jit(solution)/shard_map/all_to_all | solution.py:202
  70.6 0.6 reduce_sum.9
Async XLA Ops:
  0.0 13.0 %collective-permute-start.1 = (bf16[128,512]{1,0:T(8,128)(2,1)}, bf16[128,512]{1,0:T(8,128)(2,1)S(1)}, u32[]{:S(2)}, u32[]{:S(2)}) collective-permute-start(bf16[128,512]{1,0:T(8,128)(2,1)} %mode2_ref.1), channel_id=1, source_target_pairs={{0,2},{2,0},{4,6},{6,4},{1,3},{3,1},{5,7},{7,5},{8,10},{10,8},{12,... | collective-permute-start | bytes 393224 | tf_op jit(solution)/shard_map/ppermute | solution.py:21
  3.1 12.5 %collective-permute-start.8 = (bf16[128,512]{1,0:T(8,128)(2,1)}, bf16[128,512]{1,0:T(8,128)(2,1)S(1)}, u32[]{:S(2)}, u32[]{:S(2)}) collective-permute-start(bf16[128,512]{1,0:T(8,128)(2,1)} %mode3_ref.1), channel_id=1, source_target_pairs={{0,16},{16,0},{1,17},{17,1},{2,18},{18,2},{3,19},{19,3},{4,20},{20... | collective-permute-start | bytes 393224 | tf_op jit(solution)/shard_map/ppermute | solution.py:21
  4.5 11.5 %collective-permute-start.7 = (bf16[128,512]{1,0:T(8,128)(2,1)}, bf16[128,512]{1,0:T(8,128)(2,1)S(1)}, u32[]{:S(2)}, u32[]{:S(2)}) collective-permute-start(bf16[128,512]{1,0:T(8,128)(2,1)} %mode3_ref.1), channel_id=1, source_target_pairs={{0,8},{8,0},{1,9},{9,1},{2,10},{10,2},{3,11},{11,3},{4,12},{12,4},... | collective-permute-start | bytes 393224 | tf_op jit(solution)/shard_map/ppermute | solution.py:21
  4.5 14.8 %collective-permute-start = (bf16[128,512]{1,0:T(8,128)(2,1)}, bf16[128,512]{1,0:T(8,128)(2,1)S(1)}, u32[]{:S(2)}, u32[]{:S(2)}) collective-permute-start(bf16[128,512]{1,0:T(8,128)(2,1)} %mode2_ref.1), channel_id=1, source_target_pairs={{0,1},{1,0},{2,3},{3,2},{4,5},{5,4},{6,7},{7,6},{8,9},{9,8},{10,11... | collective-permute-start | bytes 393224 | tf_op jit(solution)/shard_map/ppermute | solution.py:21
  6.1 9.5 %collective-permute-start.3 = (bf16[128,512]{1,0:T(8,128)(2,1)}, bf16[128,512]{1,0:T(8,128)(2,1)S(1)}, u32[]{:S(2)}, u32[]{:S(2)}) collective-permute-start(bf16[128,512]{1,0:T(8,128)(2,1)} %mode2_ref.1), channel_id=1, source_target_pairs={{0,4},{2,6},{4,0},{6,2},{1,5},{3,7},{5,1},{7,3},{8,12},{10,14},{12... | collective-permute-start | bytes 393224 | tf_op jit(solution)/shard_map/ppermute | solution.py:21
  9.3 4.2 %copy-start.2 = (s32[4,3]{1,0:T(4,128)S(1)}, s32[4,3]{1,0:T(4,128)}, u32[]{:S(2)}) copy-start(s32[4,3]{1,0:T(4,128)} %param.6) | copy-start | bytes 148
  11.0 1.9 %copy-start = (bf16[2,64,128,128]{3,2,1,0:T(8,128)(2,1)}, bf16[2,64,128,128]{3,2,1,0:T(8,128)(2,1)S(1)}, u32[]{:S(2)}) copy-start(bf16[2,64,128,128]{3,2,1,0:T(8,128)(2,1)S(1)} %get-tuple-element.14.refs_12_) | copy-start | bytes 12582916
  13.0 5.5 %collective-permute-start.2 = (bf16[128,512]{1,0:T(8,128)(2,1)S(1)}, bf16[128,512]{1,0:T(8,128)(2,1)S(1)}, u32[]{:S(2)}, u32[]{:S(2)}) collective-permute-start(bf16[128,512]{1,0:T(8,128)(2,1)S(1)} %collective-permute-done.1.refs_2_), channel_id=1, source_target_pairs={{0,1},{1,0},{2,3},{3,2},{4,5},{5,4},{6,7},{7,6},{8,9},{9,8},{10,11... | collective-permute-start | bytes 393224 | tf_op jit(solution)/shard_map/ppermute | solution.py:21
  15.5 5.5 %collective-permute-start.5 = (bf16[128,512]{1,0:T(8,128)(2,1)S(1)}, bf16[128,512]{1,0:T(8,128)(2,1)S(1)}, u32[]{:S(2)}, u32[]{:S(2)}) collective-permute-start(bf16[128,512]{1,0:T(8,128)(2,1)S(1)} %collective-permute-done.3.refs_4_), channel_id=1, source_target_pairs={{0,2},{2,0},{4,6},{6,4},{1,3},{3,1},{5,7},{7,5},{8,10},{10,8},{12,... | collective-permute-start | bytes 393224 | tf_op jit(solution)/shard_map/ppermute | solution.py:21
  15.5 5.6 %collective-permute-start.4 = (bf16[128,512]{1,0:T(8,128)(2,1)S(1)}, bf16[128,512]{1,0:T(8,128)(2,1)S(1)}, u32[]{:S(2)}, u32[]{:S(2)}) collective-permute-start(bf16[128,512]{1,0:T(8,128)(2,1)S(1)} %collective-permute-done.3.refs_4_), channel_id=1, source_target_pairs={{0,1},{1,0},{2,3},{3,2},{4,5},{5,4},{6,7},{7,6},{8,9},{9,8},{10,11... | collective-permute-start | bytes 393224 | tf_op jit(solution)/shard_map/ppermute | solution.py:21
  16.1 3.2 %collective-permute-start.9 = (bf16[128,512]{1,0:T(8,128)(2,1)S(1)}, bf16[128,512]{1,0:T(8,128)(2,1)S(1)}, u32[]{:S(2)}, u32[]{:S(2)}) collective-permute-start(bf16[128,512]{1,0:T(8,128)(2,1)S(1)} %collective-permute-done.8.refs_10_), channel_id=1, source_target_pairs={{0,8},{8,0},{1,9},{9,1},{2,10},{10,2},{3,11},{11,3},{4,12},{12,4},... | collective-permute-start | bytes 393224 | tf_op jit(solution)/shard_map/ppermute | solution.py:21
  18.5 8.0 %collective-permute-start.6 = (bf16[128,512]{1,0:T(8,128)(2,1)S(1)}, bf16[128,512]{1,0:T(8,128)(2,1)S(1)}, u32[]{:S(2)}, u32[]{:S(2)}) collective-permute-start(bf16[128,512]{1,0:T(8,128)(2,1)S(1)} %collective-permute-done.2.refs_3_), channel_id=1, source_target_pairs={{0,4},{2,6},{4,0},{6,2},{1,5},{3,7},{5,1},{7,3},{8,12},{10,14},{12... | collective-permute-start | bytes 393224 | tf_op jit(solution)/shard_map/ppermute | solution.py:21
  26.5 2.2 %copy-start.1 = (bf16[2,64,128,128]{3,2,1,0:T(8,128)(2,1)S(1)}, bf16[2,64,128,128]{3,2,1,0:T(8,128)(2,1)}, u32[]{:S(2)}) copy-start(bf16[2,64,128,128]{3,2,1,0:T(8,128)(2,1)} %copy-done) | copy-start | bytes 12582916
  34.5 5.9 %collective-permute-start.10 = (f32[16,16,512]{2,1,0:T(8,128)S(1)}, f32[16,16,512]{2,1,0:T(8,128)S(1)}, u32[]{:S(2)}, u32[]{:S(2)}) collective-permute-start(f32[16,16,512]{2,1,0:T(8,128)S(1)} %get-tuple-element.18), channel_id=1, source_target_pairs={{0,8},{8,0},{1,9},{9,1},{2,10},{10,2},{3,11},{11,3},{4,12},{12,4},... | collective-permute-start | bytes 1572872 | tf_op jit(solution)/shard_map/ppermute | solution.py:21

commit v3 on v2

--- a/solution.py
+++ b/solution.py
@@ -12,6 +12,12 @@
 IROWS_DEV = 16
 CORES = 2
 STEP_ROWS = 64
+LANES = 128
+SUBLANES = 8
+WIRE = jnp.float16
+WIRE_EXPONENT = 14.0
+LEAST_EXPONENT = -100.0
+LEAST = 1e-37
 PLACES = ("x", "core", "z", "y")
 CHIPS = ("x", "z", "y")
 
@@ -136,10 +142,23 @@
 
         def add_to(ref):
             for piece in range(STEP_ROWS // IROWS_DEV):
-                ref[chip + piece] += part[piece * IROWS_DEV : (piece + 1) * IROWS_DEV]
+                for tile in range(rank // LANES):
+                    ref[chip + piece, tile * IROWS_DEV : (tile + 1) * IROWS_DEV] += part[
+                        piece * IROWS_DEV : (piece + 1) * IROWS_DEV,
+                        tile * LANES : (tile + 1) * LANES,
+                    ]
 
         pl.when(column % CORES == table[slot, 3])(functools.partial(add_to, kept_ref))
         pl.when(column % CORES != table[slot, 3])(functools.partial(add_to, sent_ref))
+
+    @pl.when(index == last)
+    def _():
+        for ref in (kept_ref, sent_ref):
+            bounds_at = ref.shape[1] - SUBLANES
+            most = jnp.abs(ref[:, :SUBLANES])
+            for row in range(SUBLANES, bounds_at, SUBLANES):
+                most = jnp.maximum(most, jnp.abs(ref[:, row : row + SUBLANES]))
+            ref[:, bounds_at:] = most
 
 
 def products(blocks, table, live_counts, mode2_pieces, mode3_pieces, buffers):
@@ -173,6 +192,34 @@
     return kept, sent
 
 
+def pack_kernel(kept_ref, received_ref, out_ref):
+    bounds_at = out_ref.shape[1] - SUBLANES
+    bound = kept_ref[:, bounds_at:] + received_ref[:, bounds_at:]
+    exponent = jnp.maximum(jnp.floor(jnp.log2(jnp.maximum(bound, LEAST))), LEAST_EXPONENT)
+    scale = jnp.exp2(WIRE_EXPONENT - exponent)
+    for row in range(0, bounds_at, SUBLANES):
+        rows = slice(row, row + SUBLANES)
+        out_ref[:, rows] = (kept_ref[:, rows] + received_ref[:, rows]) * scale
+    out_ref[:, bounds_at:] = exponent
+
+
+def sum_kernel(arrived_ref, out_ref):
+    bounds_at = arrived_ref.shape[1] - SUBLANES
+    scale = jnp.exp2(arrived_ref[:, bounds_at:] - WIRE_EXPONENT)
+    for row in range(0, bounds_at, SUBLANES):
+        tile, place = divmod(row, IROWS_DEV)
+        total = (arrived_ref[:, row : row + SUBLANES] * scale).sum(axis=0)
+        out_ref[place : place + SUBLANES, tile * LANES : (tile + 1) * LANES] = total
+
+
+def small_call(kernel, out_shape):
+    return pl.pallas_call(
+        kernel,
+        out_shape=jax.ShapeDtypeStruct(out_shape, jnp.float32),
+        compiler_params=pltpu.CompilerParams(vmem_limit_bytes=16 << 20),
+    )
+
+
 def on_device(blocks, coords, live_counts, mode2_factor, mode3_factor):
     x, core, z, y = (lax.axis_index(axis) for axis in PLACES)
     n_ja, n_ka = lax.axis_size(("x", "core")), lax.axis_size(("z", "y"))
@@ -188,7 +235,8 @@
     mode2_pieces = gather_pieces(mode2_factor, "z", "y")
     mode3_pieces = gather_pieces(mode3_factor, "x", "core")
     blocks = pltpu.with_memory_space_constraint(blocks, pltpu.HBM)
-    half_shape = (n_ja * n_ka // CORES, IROWS_DEV, mode2_factor.shape[1])
+    rank = mode2_factor.shape[1]
+    half_shape = (n_ja * n_ka // CORES, rank // LANES * IROWS_DEV + SUBLANES, LANES)
     cubes, mode2_pieces[0], mode3_pieces[0], kept, sent = fetch_local(
         blocks,
         pltpu.with_memory_space_constraint(mode2_factor, pltpu.HBM),
@@ -199,8 +247,9 @@
         blocks, table, live_counts, mode2_pieces, mode3_pieces, (cubes, kept, sent)
     )
     received = exchange(sent, "core", 1)
-    arrived = lax.all_to_all(kept + received, CHIPS, 0, 0, tiled=True)
-    return arrived.sum(axis=0)
+    packed = small_call(pack_kernel, half_shape)(kept, received).astype(WIRE)
+    arrived = lax.all_to_all(packed, CHIPS, 0, 0, tiled=True).astype(jnp.float32)
+    return small_call(sum_kernel, (IROWS_DEV, rank))(arrived)
 
 
 def solution(mesh):

time: 71.5 us -> 67.3 us (0.941)
  blocking collectives: 30.2 us -> 25.6 us
  Pallas kernels: 7.39 us -> 8.23 us
    all_to_all x1, blocking collectives: 30.2 us -> 25.6 us  [on_device(): lax.all_to_all(packed, CHIPS, 0, 0, tiled=True).astype(jnp.float32)]
    pallas_call x0 -> x2, Pallas kernels: none -> 0.73 us  [the longest x1 0.67 us: on_device(): return small_call(sum_kernel, (IROWS_DEV, rank))(arrived)]
where the time goes in v3:
time: 67.3 us; the launch traced here: 67 us
  blocking collectives  25.6 us (38%)
  starting transfers between devices  14.8 us (22%)
  waiting for transfers between devices  13.2 us (20%)
  Pallas kernels  8.23 us (12%)
  local copies, waits for them, and re-layouts  4.23 us (6%)
  between operations  0.71 us (1%)
    all_to_all x1, blocking collectives, on_device(): lax.all_to_all(packed, CHIPS, 0, 0, tiled=True).astype(jnp.float32)  25.6 us
    ppermute x11, starting transfers between devices, exchange(): return lax.ppermute(value, axis, [(i, i ^ code) for i in range(size)])  14.8 us
    ppermute x11, waiting for transfers between devices, exchange(): return lax.ppermute(value, axis, [(i, i ^ code) for i in range(size)])  13.2 us
    pallas_call x1, Pallas kernels, products(): pl.pallas_call(functools.partial(product_kernel, n_ja, n_ka, steps), out_...  5.87 us
    unnamed x6, local copies, waits for them, and re-layouts  4.15 us
    pallas_call x1, Pallas kernels, fetch_local(): pl.pallas_call(fetch_kernel, out_shape=[jax.ShapeDtypeStruct((2, STEP_ROW...  1.63 us
  transfers between devices with their start and end apart: 11, of which 6 were waited for; matrix products, arithmetic and copies ran while one was open for 0% of the time, Pallas kernels for 2%

profile of v3, /device:TPU:0, one launch (start us, length us, event | category | flops | bytes accessed | tf_op | source)
XLA Modules:
  0.0 67.0 jit_solution(14434841726935298318)
XLA Ops:
  0.0 3.1 %collective-permute-start.1 = (bf16[128,512]{1,0:T(8,128)(2,1)}, bf16[128,512]{1,0:T(8,128)(2,1)S(1)}, u32[]{:S(2)}, u32[]{:S(2)}) collective-permute-start(bf16[128,512]{1,0:T(8,128)(2,1)} %mode2_ref.1), channel_id=1, source_target_pairs={{0,2},{2,0},{4,6},{6,4},{1,3},{3,1},{5,7},{7,5},{8,10},{10,8},{12,... | collective-permute-start | bytes 393224 | tf_op jit(solution)/shard_map/ppermute | solution.py:27
  3.1 1.5 %collective-permute-start.8 = (bf16[128,512]{1,0:T(8,128)(2,1)}, bf16[128,512]{1,0:T(8,128)(2,1)S(1)}, u32[]{:S(2)}, u32[]{:S(2)}) collective-permute-start(bf16[128,512]{1,0:T(8,128)(2,1)} %mode3_ref.1), channel_id=1, source_target_pairs={{0,16},{16,0},{1,17},{17,1},{2,18},{18,2},{3,19},{19,3},{4,20},{20... | collective-permute-start | bytes 393224 | tf_op jit(solution)/shard_map/ppermute | solution.py:27
  4.5 0.0 collective-permute-start.7
  4.5 1.5 %collective-permute-start = (bf16[128,512]{1,0:T(8,128)(2,1)}, bf16[128,512]{1,0:T(8,128)(2,1)S(1)}, u32[]{:S(2)}, u32[]{:S(2)}) collective-permute-start(bf16[128,512]{1,0:T(8,128)(2,1)} %mode2_ref.1), channel_id=1, source_target_pairs={{0,1},{1,0},{2,3},{3,2},{4,5},{5,4},{6,7},{7,6},{8,9},{9,8},{10,11... | collective-permute-start | bytes 393224 | tf_op jit(solution)/shard_map/ppermute | solution.py:27
  6.1 2.6 %collective-permute-start.3 = (bf16[128,512]{1,0:T(8,128)(2,1)}, bf16[128,512]{1,0:T(8,128)(2,1)S(1)}, u32[]{:S(2)}, u32[]{:S(2)}) collective-permute-start(bf16[128,512]{1,0:T(8,128)(2,1)} %mode2_ref.1), channel_id=1, source_target_pairs={{0,4},{2,6},{4,0},{6,2},{1,5},{3,7},{5,1},{7,3},{8,12},{10,14},{12... | collective-permute-start | bytes 393224 | tf_op jit(solution)/shard_map/ppermute | solution.py:27
  9.3 0.0 copy-start.2
  9.3 1.6 %shard_map.55 = (bf16[2,64,128,128]{3,2,1,0:T(8,128)(2,1)S(1)}, bf16[128,512]{1,0:T(8,128)(2,1)S(1)}, bf16[128,512]{1,0:T(8,128)(2,1)S(1)}, f32[16,72,128]{2,1,0:T(8,128)S(1)}, f32[16,72,128]{2,1,0:T(8,128)S(1)}) custom-call(bf16[4,128,128,128]{3,2,1,0:T(8,128)(2,1)} %blocks_ref.3, bf16[128,512]{1,0:T(8,128)(2,1)} %mode2_ref.1, bf16[128,512]{1,0:T(8,128)(2,1)} %mode3_ref.1), custom_call_target="tpu_custom_call" | custom-call | bytes 4194304 | tf_op jit(solution)/shard_map/pallas_call | solution.py:81
  11.0 0.0 copy-start
  11.0 2.0 %copy-done = bf16[2,64,128,128]{3,2,1,0:T(8,128)(2,1)} copy-done((bf16[2,64,128,128]{3,2,1,0:T(8,128)(2,1)}, bf16[2,64,128,128]{3,2,1,0:T(8,128)(2,1)S(1)}, u32[]{:S(2)}) %copy-start) | copy-done | bytes 4194328
  12.9 0.1 pad.3.clone
  13.0 0.0 collective-permute-done.1.refs_2_
  13.0 0.5 collective-permute-start.2
  13.5 0.0 copy-done.2
  13.5 0.1 fusion.4
  13.6 1.9 %collective-permute-done.3.refs_4_ = bf16[128,512]{1,0:T(8,128)(2,1)S(1)} collective-permute-done((bf16[128,512]{1,0:T(8,128)(2,1)}, bf16[128,512]{1,0:T(8,128)(2,1)S(1)}, u32[]{:S(2)}, u32[]{:S(2)}) %collective-permute-start.3) | collective-permute-done | bytes 131104 | tf_op jit(solution)/shard_map/ppermute | solution.py:27
  15.5 0.0 collective-permute-start.5
  15.5 0.0 collective-permute-done.8.refs_10_
  15.5 0.6 collective-permute-start.4
  16.1 0.0 collective-permute-done.7.refs_9_
  16.1 0.0 collective-permute-start.9
  16.1 2.4 %collective-permute-done.2.refs_3_ = bf16[128,512]{1,0:T(8,128)(2,1)S(1)} collective-permute-done((bf16[128,512]{1,0:T(8,128)(2,1)S(1)}, bf16[128,512]{1,0:T(8,128)(2,1)S(1)}, u32[]{:S(2)}, u32[]{:S(2)}) %collective-permute-start.2) | collective-permute-done | bytes 131104 | tf_op jit(solution)/shard_map/ppermute | solution.py:27
  18.5 0.7 %collective-permute-start.6 = (bf16[128,512]{1,0:T(8,128)(2,1)S(1)}, bf16[128,512]{1,0:T(8,128)(2,1)S(1)}, u32[]{:S(2)}, u32[]{:S(2)}) collective-permute-start(bf16[128,512]{1,0:T(8,128)(2,1)S(1)} %collective-permute-done.2.refs_3_), channel_id=1, source_target_pairs={{0,4},{2,6},{4,0},{6,2},{1,5},{3,7},{5,1},{7,3},{8,12},{10,14},{12... | collective-permute-start | bytes 393224 | tf_op jit(solution)/shard_map/ppermute | solution.py:27
  19.2 0.1 add_add_fusion.table
  19.3 0.0 collective-permute-done.refs_1_
  19.3 0.0 collective-permute-done.9.refs_11_
  19.3 1.7 %collective-permute-done.5.refs_6_ = bf16[128,512]{1,0:T(8,128)(2,1)S(1)} collective-permute-done((bf16[128,512]{1,0:T(8,128)(2,1)S(1)}, bf16[128,512]{1,0:T(8,128)(2,1)S(1)}, u32[]{:S(2)}, u32[]{:S(2)}) %collective-permute-start.5) | collective-permute-done | bytes 131104 | tf_op jit(solution)/shard_map/ppermute | solution.py:27
  21.0 0.2 collective-permute-done.4.refs_5_
  21.2 5.4 %collective-permute-done.6.refs_7_ = bf16[128,512]{1,0:T(8,128)(2,1)S(1)} collective-permute-done((bf16[128,512]{1,0:T(8,128)(2,1)S(1)}, bf16[128,512]{1,0:T(8,128)(2,1)S(1)}, u32[]{:S(2)}, u32[]{:S(2)}) %collective-permute-start.6) | collective-permute-done | bytes 131104 | tf_op jit(solution)/shard_map/ppermute | solution.py:27
  26.6 0.0 copy-start.1
  26.6 2.2 %copy-done.1 = bf16[2,64,128,128]{3,2,1,0:T(8,128)(2,1)S(1)} copy-done((bf16[2,64,128,128]{3,2,1,0:T(8,128)(2,1)S(1)}, bf16[2,64,128,128]{3,2,1,0:T(8,128)(2,1)}, u32[]{:S(2)}) %copy-start.1) | copy-done | bytes 4194328
  28.7 5.9 %shard_map.56 = (bf16[2,64,128,128]{3,2,1,0:T(8,128)(2,1)S(1)}, f32[16,72,128]{2,1,0:T(8,128)S(1)}, f32[16,72,128]{2,1,0:T(8,128)S(1)}) custom-call(s32[4,4]{1,0:T(4,128)S(1)} %add_add_fusion.table, s32[1]{0:T(128)S(6)} %copy.12.live, bf16[4,128,128,128]{3,2,1,0:T(8,128)(2,1)} %blocks_ref.3, ...), custom_call_target="tpu_custom_call", output_to_operand_aliasing={{0}: (15, {}), {1}: (16, {}), {2}: (17, {})} | custom-call | flops 8589934592 | bytes 16777216 | tf_op jit(solution)/shard_map/pallas_call | solution.py:172
  34.6 4.3 %collective-permute-start.10 = (f32[16,72,128]{2,1,0:T(8,128)S(1)}, f32[16,72,128]{2,1,0:T(8,128)S(1)}, u32[]{:S(2)}, u32[]{:S(2)}) collective-permute-start(f32[16,72,128]{2,1,0:T(8,128)S(1)} %get-tuple-element.18), channel_id=1, source_target_pairs={{0,8},{8,0},{1,9},{9,1},{2,10},{10,2},{3,11},{11,3},{4,12},{12,4},... | collective-permute-start | bytes 1769480 | tf_op jit(solution)/shard_map/ppermute | solution.py:27
  39.0 1.6 %collective-permute-done.10.received_ref = f32[16,72,128]{2,1,0:T(8,128)S(1)} collective-permute-done((f32[16,72,128]{2,1,0:T(8,128)S(1)}, f32[16,72,128]{2,1,0:T(8,128)S(1)}, u32[]{:S(2)}, u32[]{:S(2)}) %collective-permute-start.10) | collective-permute-done | bytes 589856 | tf_op jit(solution)/shard_map/ppermute | solution.py:27
  40.6 0.1 shard_map.57
  40.7 25.6 %all_to_all.5 = f16[16,72,128]{2,1,0:T(8,128)(2,1)S(1)} all-to-all(f16[16,72,128]{2,1,0:T(8,128)(2,1)S(1)} %convert_element_type.6), channel_id=1, replica_groups=mesh['x'=2,'core'=2,'z'=4,'y'=2] {'x','z','y'}, dimensions={0} | all-to-all | bytes 589824 | tf_op jit(solution)/shard_map/all_to_all | solution.py:251
  66.4 0.7 shard_map.58
  (2 shorter events, 0.1 us)
Async XLA Ops:
  0.0 13.0 %collective-permute-start.1 = (bf16[128,512]{1,0:T(8,128)(2,1)}, bf16[128,512]{1,0:T(8,128)(2,1)S(1)}, u32[]{:S(2)}, u32[]{:S(2)}) collective-permute-start(bf16[128,512]{1,0:T(8,128)(2,1)} %mode2_ref.1), channel_id=1, source_target_pairs={{0,2},{2,0},{4,6},{6,4},{1,3},{3,1},{5,7},{7,5},{8,10},{10,8},{12,... | collective-permute-start | bytes 393224 | tf_op jit(solution)/shard_map/ppermute | solution.py:27
  3.1 12.5 %collective-permute-start.8 = (bf16[128,512]{1,0:T(8,128)(2,1)}, bf16[128,512]{1,0:T(8,128)(2,1)S(1)}, u32[]{:S(2)}, u32[]{:S(2)}) collective-permute-start(bf16[128,512]{1,0:T(8,128)(2,1)} %mode3_ref.1), channel_id=1, source_target_pairs={{0,16},{16,0},{1,17},{17,1},{2,18},{18,2},{3,19},{19,3},{4,20},{20... | collective-permute-start | bytes 393224 | tf_op jit(solution)/shard_map/ppermute | solution.py:27
  4.5 11.5 %collective-permute-start.7 = (bf16[128,512]{1,0:T(8,128)(2,1)}, bf16[128,512]{1,0:T(8,128)(2,1)S(1)}, u32[]{:S(2)}, u32[]{:S(2)}) collective-permute-start(bf16[128,512]{1,0:T(8,128)(2,1)} %mode3_ref.1), channel_id=1, source_target_pairs={{0,8},{8,0},{1,9},{9,1},{2,10},{10,2},{3,11},{11,3},{4,12},{12,4},... | collective-permute-start | bytes 393224 | tf_op jit(solution)/shard_map/ppermute | solution.py:27
  4.5 14.8 %collective-permute-start = (bf16[128,512]{1,0:T(8,128)(2,1)}, bf16[128,512]{1,0:T(8,128)(2,1)S(1)}, u32[]{:S(2)}, u32[]{:S(2)}) collective-permute-start(bf16[128,512]{1,0:T(8,128)(2,1)} %mode2_ref.1), channel_id=1, source_target_pairs={{0,1},{1,0},{2,3},{3,2},{4,5},{5,4},{6,7},{7,6},{8,9},{9,8},{10,11... | collective-permute-start | bytes 393224 | tf_op jit(solution)/shard_map/ppermute | solution.py:27
  6.1 9.5 %collective-permute-start.3 = (bf16[128,512]{1,0:T(8,128)(2,1)}, bf16[128,512]{1,0:T(8,128)(2,1)S(1)}, u32[]{:S(2)}, u32[]{:S(2)}) collective-permute-start(bf16[128,512]{1,0:T(8,128)(2,1)} %mode2_ref.1), channel_id=1, source_target_pairs={{0,4},{2,6},{4,0},{6,2},{1,5},{3,7},{5,1},{7,3},{8,12},{10,14},{12... | collective-permute-start | bytes 393224 | tf_op jit(solution)/shard_map/ppermute | solution.py:27
  9.3 4.2 %copy-start.2 = (s32[4,3]{1,0:T(4,128)S(1)}, s32[4,3]{1,0:T(4,128)}, u32[]{:S(2)}) copy-start(s32[4,3]{1,0:T(4,128)} %param.6) | copy-start | bytes 148
  11.0 2.0 %copy-start = (bf16[2,64,128,128]{3,2,1,0:T(8,128)(2,1)}, bf16[2,64,128,128]{3,2,1,0:T(8,128)(2,1)S(1)}, u32[]{:S(2)}) copy-start(bf16[2,64,128,128]{3,2,1,0:T(8,128)(2,1)S(1)} %get-tuple-element.14.refs_12_) | copy-start | bytes 12582916
  13.0 5.5 %collective-permute-start.2 = (bf16[128,512]{1,0:T(8,128)(2,1)S(1)}, bf16[128,512]{1,0:T(8,128)(2,1)S(1)}, u32[]{:S(2)}, u32[]{:S(2)}) collective-permute-start(bf16[128,512]{1,0:T(8,128)(2,1)S(1)} %collective-permute-done.1.refs_2_), channel_id=1, source_target_pairs={{0,1},{1,0},{2,3},{3,2},{4,5},{5,4},{6,7},{7,6},{8,9},{9,8},{10,11... | collective-permute-start | bytes 393224 | tf_op jit(solution)/shard_map/ppermute | solution.py:27
  15.5 5.5 %collective-permute-start.5 = (bf16[128,512]{1,0:T(8,128)(2,1)S(1)}, bf16[128,512]{1,0:T(8,128)(2,1)S(1)}, u32[]{:S(2)}, u32[]{:S(2)}) collective-permute-start(bf16[128,512]{1,0:T(8,128)(2,1)S(1)} %collective-permute-done.3.refs_4_), channel_id=1, source_target_pairs={{0,2},{2,0},{4,6},{6,4},{1,3},{3,1},{5,7},{7,5},{8,10},{10,8},{12,... | collective-permute-start | bytes 393224 | tf_op jit(solution)/shard_map/ppermute | solution.py:27
  15.5 5.6 %collective-permute-start.4 = (bf16[128,512]{1,0:T(8,128)(2,1)S(1)}, bf16[128,512]{1,0:T(8,128)(2,1)S(1)}, u32[]{:S(2)}, u32[]{:S(2)}) collective-permute-start(bf16[128,512]{1,0:T(8,128)(2,1)S(1)} %collective-permute-done.3.refs_4_), channel_id=1, source_target_pairs={{0,1},{1,0},{2,3},{3,2},{4,5},{5,4},{6,7},{7,6},{8,9},{9,8},{10,11... | collective-permute-start | bytes 393224 | tf_op jit(solution)/shard_map/ppermute | solution.py:27
  16.1 3.2 %collective-permute-start.9 = (bf16[128,512]{1,0:T(8,128)(2,1)S(1)}, bf16[128,512]{1,0:T(8,128)(2,1)S(1)}, u32[]{:S(2)}, u32[]{:S(2)}) collective-permute-start(bf16[128,512]{1,0:T(8,128)(2,1)S(1)} %collective-permute-done.8.refs_10_), channel_id=1, source_target_pairs={{0,8},{8,0},{1,9},{9,1},{2,10},{10,2},{3,11},{11,3},{4,12},{12,4},... | collective-permute-start | bytes 393224 | tf_op jit(solution)/shard_map/ppermute | solution.py:27
  18.5 8.0 %collective-permute-start.6 = (bf16[128,512]{1,0:T(8,128)(2,1)S(1)}, bf16[128,512]{1,0:T(8,128)(2,1)S(1)}, u32[]{:S(2)}, u32[]{:S(2)}) collective-permute-start(bf16[128,512]{1,0:T(8,128)(2,1)S(1)} %collective-permute-done.2.refs_3_), channel_id=1, source_target_pairs={{0,4},{2,6},{4,0},{6,2},{1,5},{3,7},{5,1},{7,3},{8,12},{10,14},{12... | collective-permute-start | bytes 393224 | tf_op jit(solution)/shard_map/ppermute | solution.py:27
  26.6 2.2 %copy-start.1 = (bf16[2,64,128,128]{3,2,1,0:T(8,128)(2,1)S(1)}, bf16[2,64,128,128]{3,2,1,0:T(8,128)(2,1)}, u32[]{:S(2)}) copy-start(bf16[2,64,128,128]{3,2,1,0:T(8,128)(2,1)} %copy-done) | copy-start | bytes 12582916
  34.6 6.0 %collective-permute-start.10 = (f32[16,72,128]{2,1,0:T(8,128)S(1)}, f32[16,72,128]{2,1,0:T(8,128)S(1)}, u32[]{:S(2)}, u32[]{:S(2)}) collective-permute-start(f32[16,72,128]{2,1,0:T(8,128)S(1)} %get-tuple-element.18), channel_id=1, source_target_pairs={{0,8},{8,0},{1,9},{9,1},{2,10},{10,2},{3,11},{11,3},{4,12},{12,4},... | collective-permute-start | bytes 1769480 | tf_op jit(solution)/shard_map/ppermute | solution.py:27

commit v4 on v3

--- a/solution.py
+++ b/solution.py
@@ -49,18 +49,37 @@
     return [pieces[code] for code in sorted(pieces)]
 
 
-def block_of(blocks_ref, index, steps):
-    rows = pl.ds(index % steps * STEP_ROWS, STEP_ROWS)
-    return blocks_ref.at[index // steps, rows]
-
-
-def fetch_kernel(blocks_ref, mode2_ref, mode3_ref, *refs):
+def is_late(far_code, near_code):
+    return far_code >= 2 and (near_code > 0 or far_code & (far_code - 1) > 0)
+
+
+def early_slot(table, live, early_codes):
+    slots = table.shape[0]
+    early = jnp.int32(slots)
+    for slot in reversed(range(slots)):
+        there = functools.reduce(jnp.logical_or, [table[slot, 1] == code for code in early_codes])
+        early = jnp.where(there & (slot < live[0]), slot, early)
+    found = early < slots
+    return jnp.where(found, early, 0), found.astype(jnp.int32)
+
+
+def slot_at(turn, early):
+    return jnp.where(turn == 0, early, jnp.where(turn <= early, turn - 1, turn))
+
+
+def block_of(blocks_ref, slot, step):
+    rows = pl.ds(step * STEP_ROWS, STEP_ROWS)
+    return blocks_ref.at[slot, rows]
+
+
+def fetch_kernel(early_codes, table, live, blocks_ref, mode2_ref, mode3_ref, *refs):
     cubes_ref, own2_ref, own3_ref, kept_ref, sent_ref, sems = refs
+    early, _ = early_slot(table, live, early_codes)
     copies = [
         pltpu.make_async_copy(source, target, sems.at[order])
         for order, (source, target) in enumerate(
             (
-                (block_of(blocks_ref, 0, 1), cubes_ref.at[0]),
+                (block_of(blocks_ref, early, 0), cubes_ref.at[0]),
                 (mode2_ref, own2_ref),
                 (mode3_ref, own3_ref),
             )
@@ -74,12 +93,12 @@
         copy.wait()
 
 
-def fetch_local(blocks, mode2_own, mode3_own, half_shape):
+def fetch_local(early_codes, table, live_counts, blocks, mode2_own, mode3_own, half_shape):
     edge = blocks.shape[1]
     in_hbm = pl.BlockSpec(memory_space=pl.ANY)
     in_place = pl.BlockSpec(memory_space=pltpu.VMEM)
     return pl.pallas_call(
-        fetch_kernel,
+        functools.partial(fetch_kernel, early_codes),
         out_shape=[
             jax.ShapeDtypeStruct((2, STEP_ROWS, edge, edge), blocks.dtype),
             jax.ShapeDtypeStruct(mode2_own.shape, mode2_own.dtype),
@@ -87,37 +106,39 @@
             jax.ShapeDtypeStruct(half_shape, jnp.float32),
             jax.ShapeDtypeStruct(half_shape, jnp.float32),
         ],
-        in_specs=[in_hbm] * 3,
+        in_specs=[pl.BlockSpec(memory_space=pltpu.SMEM)] * 2 + [in_hbm] * 3,
         out_specs=[in_place] * 5,
         scratch_shapes=[pltpu.SemaphoreType.DMA((3,))],
         cost_estimate=pl.CostEstimate(flops=0, bytes_accessed=4 << 20, transcendentals=0),
         compiler_params=pltpu.CompilerParams(vmem_limit_bytes=2 << 20),
-    )(blocks, mode2_own, mode3_own)
-
-
-def product_kernel(n_ja, n_ka, steps, table, live, blocks_ref, *refs):
-    mode2_refs, mode3_refs = refs[:n_ka], refs[n_ka : n_ka + n_ja]
-    cubes_ref, kept_ref, sent_ref, mode2, mode3, sems = refs[n_ka + n_ja + 3 :]
-    index = pl.program_id(0)
-    slot, step = index // steps, index % steps
+    )(table, live_counts, blocks, mode2_own, mode3_own)
+
+
+def product_kernel(codes, n_ka, n_ja, steps, early_codes, is_early, table, live, *refs):
+    blocks_ref, refs = refs[0], refs[1:]
+    mode2_refs, mode3_refs = refs[: len(codes)], refs[len(codes) : len(codes) + n_ja]
+    cubes_ref, kept_ref, sent_ref, mode2, mode3, sems = refs[len(codes) + n_ja + 3 :]
     edge, rank = mode2.shape
-    last = live[0] * steps - 1
+    early, found = early_slot(table, live, early_codes)
+    total = live[0] * steps
+    begin, end = (0, found * steps) if is_early else (found * steps, total)
+    index = begin + pl.program_id(0)
+    slot, step = slot_at(index // steps, early), index % steps
 
     def cubes_copy(at):
         side = at % 2
-        return pltpu.make_async_copy(
-            block_of(blocks_ref, at, steps), cubes_ref.at[side], sems.at[side]
-        )
-
-    @pl.when(index < last)
+        source = block_of(blocks_ref, slot_at(at // steps, early), at % steps)
+        return pltpu.make_async_copy(source, cubes_ref.at[side], sems.at[side])
+
+    @pl.when((index < end) & (index + 1 < total))
     def _():
         cubes_copy(index + 1).start()
 
-    @pl.when(index <= last)
+    @pl.when(index < end)
     def _():
         @pl.when(step == 0)
         def _():
-            for code, ref in enumerate(mode2_refs):
+            for code, ref in zip(codes, mode2_refs):
 
                 @pl.when(table[slot, 1] == code)
                 def _(ref=ref):
@@ -129,7 +150,7 @@
                 def _(ref=ref):
                     mode3[...] = ref[...]
 
-        @pl.when(index > 0)
+        @pl.when(index > begin)
         def _():
             cubes_copy(index).wait()
 
@@ -151,7 +172,15 @@
         pl.when(column % CORES == table[slot, 3])(functools.partial(add_to, kept_ref))
         pl.when(column % CORES != table[slot, 3])(functools.partial(add_to, sent_ref))
 
-    @pl.when(index == last)
+    if is_early:
+
+        @pl.when((index == end - 1) & (index + 1 < total))
+        def _():
+            cubes_copy(index + 1).wait()
+
+        return
+
+    @pl.when(pl.program_id(0) == pl.num_programs(0) - 1)
     def _():
         for ref in (kept_ref, sent_ref):
             bounds_at = ref.shape[1] - SUBLANES
@@ -161,20 +190,24 @@
             ref[:, bounds_at:] = most
 
 
-def products(blocks, table, live_counts, mode2_pieces, mode3_pieces, buffers):
+def products(early_codes, is_early, blocks, table, live_counts, pieces, mode3_pieces, buffers):
     slots, edge = blocks.shape[:2]
-    rank = mode2_pieces[0].shape[1]
-    n_ka, n_ja = len(mode2_pieces), len(mode3_pieces)
+    codes = early_codes if is_early else tuple(range(len(pieces)))
+    panels = [pieces[code] for code in codes] + mode3_pieces
+    rank = panels[0].shape[1]
     steps = edge // STEP_ROWS
+    turns = 1 if is_early else slots
     in_hbm = pl.BlockSpec(memory_space=pl.ANY)
     in_place = pl.BlockSpec(memory_space=pltpu.VMEM)
-    panels = mode2_pieces + mode3_pieces
-    _, kept, sent = pl.pallas_call(
-        functools.partial(product_kernel, n_ja, n_ka, steps),
+    kernel = functools.partial(
+        product_kernel, codes, len(pieces), len(mode3_pieces), steps, early_codes, is_early
+    )
+    return pl.pallas_call(
+        kernel,
         out_shape=[jax.ShapeDtypeStruct(buffer.shape, buffer.dtype) for buffer in buffers],
         grid_spec=pltpu.PrefetchScalarGridSpec(
             num_scalar_prefetch=2,
-            grid=(slots * steps,),
+            grid=(turns * steps,),
             in_specs=[in_hbm] + [in_place] * (len(panels) + len(buffers)),
             out_specs=[in_place] * len(buffers),
             scratch_shapes=[
@@ -184,12 +217,13 @@
             ],
         ),
         cost_estimate=pl.CostEstimate(
-            flops=2 * slots * edge**3 * rank, bytes_accessed=2 * blocks.size, transcendentals=0
+            flops=2 * turns * edge**3 * rank,
+            bytes_accessed=2 * turns * edge**3,
+            transcendentals=0,
         ),
         input_output_aliases={3 + len(panels) + order: order for order in range(len(buffers))},
         compiler_params=pltpu.CompilerParams(vmem_limit_bytes=40 << 20),
     )(table, live_counts, blocks, *panels, *buffers)
-    return kept, sent
 
 
 def pack_kernel(kept_ref, received_ref, out_ref):
@@ -237,15 +271,21 @@
     blocks = pltpu.with_memory_space_constraint(blocks, pltpu.HBM)
     rank = mode2_factor.shape[1]
     half_shape = (n_ja * n_ka // CORES, rank // LANES * IROWS_DEV + SUBLANES, LANES)
+    near_size = lax.axis_size("y")
+    early_codes = tuple(code for code in range(n_ka) if not is_late(*divmod(code, near_size)))
     cubes, mode2_pieces[0], mode3_pieces[0], kept, sent = fetch_local(
+        early_codes,
+        table,
+        live_counts,
         blocks,
         pltpu.with_memory_space_constraint(mode2_factor, pltpu.HBM),
         pltpu.with_memory_space_constraint(mode3_factor, pltpu.HBM),
         half_shape,
     )
-    kept, sent = products(
-        blocks, table, live_counts, mode2_pieces, mode3_pieces, (cubes, kept, sent)
-    )
+    product = functools.partial(products, early_codes)
+    args = blocks, table, live_counts, mode2_pieces, mode3_pieces
+    buffers = product(True, *args, (cubes, kept, sent))
+    _, kept, sent = product(False, *args, buffers)
     received = exchange(sent, "core", 1)
     packed = small_call(pack_kernel, half_shape)(kept, received).astype(WIRE)
     arrived = lax.all_to_all(packed, CHIPS, 0, 0, tiled=True).astype(jnp.float32)

time: 67.3 us -> 60.8 us (0.903)
  waiting for transfers between devices: 13.2 us -> 6.76 us
  local copies, waits for them, and re-layouts: 4.23 us -> 0.07 us
  starting transfers between devices: 14.8 us -> 17 us
  Pallas kernels: 8.23 us -> 9.86 us
  other arithmetic: 0.24 us -> 1.03 us
    ppermute x11, waiting for transfers between devices: 13.2 us -> 6.76 us  [exchange(): return lax.ppermute(value, axis, [(i, i ^ code) for i in range(size)])]
    unnamed x6 -> x0, local copies, waits for them, and re-layouts: 4.15 us -> none
    ppermute x11, starting transfers between devices: 14.8 us -> 17 us  [exchange(): return lax.ppermute(value, axis, [(i, i ^ code) for i in range(size)])]
    pallas_call x2 -> x3, Pallas kernels: 7.5 us -> 9.12 us  [the longest x2 6.91 us: products(): pl.pallas_call(kernel, out_shape=[jax.ShapeDtypeStruct(buffer.shape, buff...]
    slice x1, other arithmetic: 0.08 us -> 0.87 us  [on_device(): coords[:, 0]]
  transfers between devices with their start and end apart: 11 -> 11, of which waited for: 6 -> 3; matrix products, arithmetic and copies ran while one was open for 0% -> 2% of each run, Pallas kernels for 2% -> 13%
where the time goes in v4:
time: 60.8 us; the launch traced here: 60.6 us
  blocking collectives  25.1 us (41%)
  starting transfers between devices  17 us (28%)
  Pallas kernels  9.86 us (16%)
  waiting for transfers between devices  6.76 us (11%)
  other arithmetic  1.03 us (2%)
  between operations  0.74 us (1%)
    all_to_all x1, blocking collectives, on_device(): lax.all_to_all(packed, CHIPS, 0, 0, tiled=True).astype(jnp.float32)  25.1 us
    ppermute x11, starting transfers between devices, exchange(): return lax.ppermute(value, axis, [(i, i ^ code) for i in range(size)])  17 us
    pallas_call x2, Pallas kernels, products(): pl.pallas_call(kernel, out_shape=[jax.ShapeDtypeStruct(buffer.shape, buff...  6.91 us
    ppermute x11, waiting for transfers between devices, exchange(): return lax.ppermute(value, axis, [(i, i ^ code) for i in range(size)])  6.76 us
    pallas_call x1, Pallas kernels, fetch_local(): pl.pallas_call(functools.partial(fetch_kernel, early_codes), out_shape=[j...  2.21 us
  transfers between devices with their start and end apart: 11, of which 3 were waited for; matrix products, arithmetic and copies ran while one was open for 2% of the time, Pallas kernels for 13%

profile of v4, /device:TPU:0, one launch (start us, length us, event | category | flops | bytes accessed | tf_op | source)
XLA Modules:
  0.0 60.6 jit_solution(10250369048063045370)
XLA Ops:
  0.0 3.0 %collective-permute-start.8 = (bf16[128,512]{1,0:T(8,128)(2,1)}, bf16[128,512]{1,0:T(8,128)(2,1)S(1)}, u32[]{:S(2)}, u32[]{:S(2)}) collective-permute-start(bf16[128,512]{1,0:T(8,128)(2,1)} %mode3_ref.1), channel_id=1, source_target_pairs={{0,16},{16,0},{1,17},{17,1},{2,18},{18,2},{3,19},{19,3},{4,20},{20... | collective-permute-start | bytes 393224 | tf_op jit(solution)/shard_map/ppermute | solution.py:27
  3.0 0.0 collective-permute-start.7
  3.0 1.5 %collective-permute-start = (bf16[128,512]{1,0:T(8,128)(2,1)}, bf16[128,512]{1,0:T(8,128)(2,1)S(1)}, u32[]{:S(2)}, u32[]{:S(2)}) collective-permute-start(bf16[128,512]{1,0:T(8,128)(2,1)} %mode2_ref.1), channel_id=1, source_target_pairs={{0,1},{1,0},{2,3},{3,2},{4,5},{5,4},{6,7},{7,6},{8,9},{9,8},{10,11... | collective-permute-start | bytes 393224 | tf_op jit(solution)/shard_map/ppermute | solution.py:27
  4.5 2.6 %collective-permute-start.3 = (bf16[128,512]{1,0:T(8,128)(2,1)}, bf16[128,512]{1,0:T(8,128)(2,1)S(1)}, u32[]{:S(2)}, u32[]{:S(2)}) collective-permute-start(bf16[128,512]{1,0:T(8,128)(2,1)} %mode2_ref.1), channel_id=1, source_target_pairs={{0,4},{2,6},{4,0},{6,2},{1,5},{3,7},{5,1},{7,3},{8,12},{10,14},{12... | collective-permute-start | bytes 393224 | tf_op jit(solution)/shard_map/ppermute | solution.py:27
  7.1 1.6 %collective-permute-start.1 = (bf16[128,512]{1,0:T(8,128)(2,1)}, bf16[128,512]{1,0:T(8,128)(2,1)S(1)}, u32[]{:S(2)}, u32[]{:S(2)}) collective-permute-start(bf16[128,512]{1,0:T(8,128)(2,1)} %mode2_ref.1), channel_id=1, source_target_pairs={{0,2},{2,0},{4,6},{6,4},{1,3},{3,1},{5,7},{7,5},{8,10},{10,8},{12,... | collective-permute-start | bytes 393224 | tf_op jit(solution)/shard_map/ppermute | solution.py:27
  9.3 0.1 pad.3.clone
  9.4 0.9 %fusion.4 = (s32[4,1]{1,0:T(4,128)S(1)}, s32[4,1]{1,0:T(4,128)S(1)}, s32[4,1]{1,0:T(4,128)S(1)}) fusion(s32[4,3]{1,0:T(4,128)} %param.6, s32[]{:T(128)S(6)} %add.7, s32[]{:T(128)S(6)} %add.6), kind=kLoop, calls=%fused_computation.9 | loop fusion | flops 56 | bytes 104 | tf_op jit(solution)/shard_map/slice | solution.py:262
  10.3 0.0 collective-permute-done.8.refs_8_.refs_11_
  10.3 0.1 collective-permute-start.9
  10.3 4.0 %collective-permute-done.1.refs_3_ = bf16[128,512]{1,0:T(8,128)(2,1)S(1)} collective-permute-done((bf16[128,512]{1,0:T(8,128)(2,1)}, bf16[128,512]{1,0:T(8,128)(2,1)S(1)}, u32[]{:S(2)}, u32[]{:S(2)}) %collective-permute-start.1) | collective-permute-done | bytes 131104 | tf_op jit(solution)/shard_map/ppermute | solution.py:27
  14.3 0.5 collective-permute-start.2
  14.8 0.1 add_add_fusion.table
  14.9 2.2 %shard_map.55 = (bf16[2,64,128,128]{3,2,1,0:T(8,128)(2,1)S(1)}, bf16[128,512]{1,0:T(8,128)(2,1)S(1)}, bf16[128,512]{1,0:T(8,128)(2,1)S(1)}, f32[16,72,128]{2,1,0:T(8,128)S(1)}, f32[16,72,128]{2,1,0:T(8,128)S(1)}) custom-call(s32[4,4]{1,0:T(4,128)S(1)} %add_add_fusion.table, s32[1]{0:T(128)S(6)} %copy.18.live, bf16[4,128,128,128]{3,2,1,0:T(8,128)(2,1)} %refs_0_.3, ...), custom_call_target="tpu_custom_call" | custom-call | bytes 4194304 | tf_op jit(solution)/shard_map/pallas_call | solution.py:100
  17.1 0.0 collective-permute-done.3.refs_5_
  17.1 1.5 %collective-permute-start.5 = (bf16[128,512]{1,0:T(8,128)(2,1)S(1)}, bf16[128,512]{1,0:T(8,128)(2,1)S(1)}, u32[]{:S(2)}, u32[]{:S(2)}) collective-permute-start(bf16[128,512]{1,0:T(8,128)(2,1)S(1)} %collective-permute-done.3.refs_5_), channel_id=1, source_target_pairs={{0,2},{2,0},{4,6},{6,4},{1,3},{3,1},{5,7},{7,5},{8,10},{10,8},{12,... | collective-permute-start | bytes 393224 | tf_op jit(solution)/shard_map/ppermute | solution.py:27
  18.6 0.0 collective-permute-done.7.refs_7_.refs_10_
  18.7 1.5 %collective-permute-start.4 = (bf16[128,512]{1,0:T(8,128)(2,1)S(1)}, bf16[128,512]{1,0:T(8,128)(2,1)S(1)}, u32[]{:S(2)}, u32[]{:S(2)}) collective-permute-start(bf16[128,512]{1,0:T(8,128)(2,1)S(1)} %collective-permute-done.3.refs_5_), channel_id=1, source_target_pairs={{0,1},{1,0},{2,3},{3,2},{4,5},{5,4},{6,7},{7,6},{8,9},{9,8},{10,11... | collective-permute-start | bytes 393224 | tf_op jit(solution)/shard_map/ppermute | solution.py:27
  20.2 0.0 collective-permute-done.2.refs_4_
  20.2 0.7 %collective-permute-start.6 = (bf16[128,512]{1,0:T(8,128)(2,1)S(1)}, bf16[128,512]{1,0:T(8,128)(2,1)S(1)}, u32[]{:S(2)}, u32[]{:S(2)}) collective-permute-start(bf16[128,512]{1,0:T(8,128)(2,1)S(1)} %collective-permute-done.2.refs_4_), channel_id=1, source_target_pairs={{0,4},{2,6},{4,0},{6,2},{1,5},{3,7},{5,1},{7,3},{8,12},{10,14},{12... | collective-permute-start | bytes 393224 | tf_op jit(solution)/shard_map/ppermute | solution.py:27
  20.8 0.0 collective-permute-done.refs_2_
  20.8 0.0 collective-permute-done.9.refs_9_.refs_12_
  20.8 5.7 %shard_map.56 = (bf16[2,64,128,128]{3,2,1,0:T(8,128)(2,1)S(1)}, f32[16,72,128]{2,1,0:T(8,128)S(1)}, f32[16,72,128]{2,1,0:T(8,128)S(1)}) custom-call(s32[4,4]{1,0:T(4,128)S(1)} %add_add_fusion.table, s32[1]{0:T(128)S(6)} %copy.18.live, bf16[4,128,128,128]{3,2,1,0:T(8,128)(2,1)} %refs_0_.3, ...), custom_call_target="tpu_custom_call", output_to_operand_aliasing={{0}: (12, {}), {1}: (13, {}), {2}: (14, {})} | custom-call | flops 2147483648 | bytes 4194304 | tf_op jit(solution)/shard_map/pallas_call | solution.py:205
  26.6 0.0 collective-permute-done.5.refs_7_
  26.6 0.0 collective-permute-done.4.refs_6_
  26.6 1.1 %collective-permute-done.6.refs_8_ = bf16[128,512]{1,0:T(8,128)(2,1)S(1)} collective-permute-done((bf16[128,512]{1,0:T(8,128)(2,1)S(1)}, bf16[128,512]{1,0:T(8,128)(2,1)S(1)}, u32[]{:S(2)}, u32[]{:S(2)}) %collective-permute-start.6) | collective-permute-done | bytes 131104 | tf_op jit(solution)/shard_map/ppermute | solution.py:27
  27.7 1.2 %shard_map.57 = (bf16[2,64,128,128]{3,2,1,0:T(8,128)(2,1)S(1)}, f32[16,72,128]{2,1,0:T(8,128)S(1)}, f32[16,72,128]{2,1,0:T(8,128)S(1)}) custom-call(s32[4,4]{1,0:T(4,128)S(1)} %add_add_fusion.table, s32[1]{0:T(128)S(6)} %copy.18.live, bf16[4,128,128,128]{3,2,1,0:T(8,128)(2,1)} %refs_0_.3, ...), custom_call_target="tpu_custom_call", output_to_operand_aliasing={{0}: (15, {}), {1}: (16, {}), {2}: (17, {})} | custom-call | flops 8589934592 | bytes 16777216 | tf_op jit(solution)/shard_map/pallas_call | solution.py:205
  28.9 4.1 %collective-permute-start.10 = (f32[16,72,128]{2,1,0:T(8,128)S(1)}, f32[16,72,128]{2,1,0:T(8,128)S(1)}, u32[]{:S(2)}, u32[]{:S(2)}) collective-permute-start(f32[16,72,128]{2,1,0:T(8,128)S(1)} %get-tuple-element.24), channel_id=1, source_target_pairs={{0,8},{8,0},{1,9},{9,1},{2,10},{10,2},{3,11},{11,3},{4,12},{12,4},... | collective-permute-start | bytes 1769480 | tf_op jit(solution)/shard_map/ppermute | solution.py:27
  33.0 1.6 %collective-permute-done.10.received_ref = f32[16,72,128]{2,1,0:T(8,128)S(1)} collective-permute-done((f32[16,72,128]{2,1,0:T(8,128)S(1)}, f32[16,72,128]{2,1,0:T(8,128)S(1)}, u32[]{:S(2)}, u32[]{:S(2)}) %collective-permute-start.10) | collective-permute-done | bytes 589856 | tf_op jit(solution)/shard_map/ppermute | solution.py:27
  34.6 0.1 shard_map.58
  34.7 25.1 %all_to_all.5 = f16[16,72,128]{2,1,0:T(8,128)(2,1)S(1)} all-to-all(f16[16,72,128]{2,1,0:T(8,128)(2,1)S(1)} %convert_element_type.6), channel_id=1, replica_groups=mesh['x'=2,'core'=2,'z'=4,'y'=2] {'x','z','y'}, dimensions={0} | all-to-all | bytes 589824 | tf_op jit(solution)/shard_map/all_to_all | solution.py:291
  59.9 0.7 %shard_map.59 = f32[16,512]{1,0:T(8,128)} custom-call(f32[16,72,128]{2,1,0:T(8,128)S(1)} %convert_element_type.7.arrived_ref), custom_call_target="tpu_custom_call" | custom-call | tf_op jit(solution)/shard_map/pallas_call | solution.py:292
  (2 shorter events, 0.1 us)
Async XLA Ops:
  0.0 10.3 %collective-permute-start.8 = (bf16[128,512]{1,0:T(8,128)(2,1)}, bf16[128,512]{1,0:T(8,128)(2,1)S(1)}, u32[]{:S(2)}, u32[]{:S(2)}) collective-permute-start(bf16[128,512]{1,0:T(8,128)(2,1)} %mode3_ref.1), channel_id=1, source_target_pairs={{0,16},{16,0},{1,17},{17,1},{2,18},{18,2},{3,19},{19,3},{4,20},{20... | collective-permute-start | bytes 393224 | tf_op jit(solution)/shard_map/ppermute | solution.py:27
  3.0 15.7 %collective-permute-start.7 = (bf16[128,512]{1,0:T(8,128)(2,1)}, bf16[128,512]{1,0:T(8,128)(2,1)S(1)}, u32[]{:S(2)}, u32[]{:S(2)}) collective-permute-start(bf16[128,512]{1,0:T(8,128)(2,1)} %mode3_ref.1), channel_id=1, source_target_pairs={{0,8},{8,0},{1,9},{9,1},{2,10},{10,2},{3,11},{11,3},{4,12},{12,4},... | collective-permute-start | bytes 393224 | tf_op jit(solution)/shard_map/ppermute | solution.py:27
  3.0 17.9 %collective-permute-start = (bf16[128,512]{1,0:T(8,128)(2,1)}, bf16[128,512]{1,0:T(8,128)(2,1)S(1)}, u32[]{:S(2)}, u32[]{:S(2)}) collective-permute-start(bf16[128,512]{1,0:T(8,128)(2,1)} %mode2_ref.1), channel_id=1, source_target_pairs={{0,1},{1,0},{2,3},{3,2},{4,5},{5,4},{6,7},{7,6},{8,9},{9,8},{10,11... | collective-permute-start | bytes 393224 | tf_op jit(solution)/shard_map/ppermute | solution.py:27
  4.5 12.6 %collective-permute-start.3 = (bf16[128,512]{1,0:T(8,128)(2,1)}, bf16[128,512]{1,0:T(8,128)(2,1)S(1)}, u32[]{:S(2)}, u32[]{:S(2)}) collective-permute-start(bf16[128,512]{1,0:T(8,128)(2,1)} %mode2_ref.1), channel_id=1, source_target_pairs={{0,4},{2,6},{4,0},{6,2},{1,5},{3,7},{5,1},{7,3},{8,12},{10,14},{12... | collective-permute-start | bytes 393224 | tf_op jit(solution)/shard_map/ppermute | solution.py:27
  7.1 7.3 %collective-permute-start.1 = (bf16[128,512]{1,0:T(8,128)(2,1)}, bf16[128,512]{1,0:T(8,128)(2,1)S(1)}, u32[]{:S(2)}, u32[]{:S(2)}) collective-permute-start(bf16[128,512]{1,0:T(8,128)(2,1)} %mode2_ref.1), channel_id=1, source_target_pairs={{0,2},{2,0},{4,6},{6,4},{1,3},{3,1},{5,7},{7,5},{8,10},{10,8},{12,... | collective-permute-start | bytes 393224 | tf_op jit(solution)/shard_map/ppermute | solution.py:27
  10.3 10.6 %collective-permute-start.9 = (bf16[128,512]{1,0:T(8,128)(2,1)S(1)}, bf16[128,512]{1,0:T(8,128)(2,1)S(1)}, u32[]{:S(2)}, u32[]{:S(2)}) collective-permute-start(bf16[128,512]{1,0:T(8,128)(2,1)S(1)} %collective-permute-done.8.refs_8_.refs_11_), channel_id=1, source_target_pairs={{0,8},{8,0},{1,9},{9,1},{2,10},{10,2},{3,11},{11,3},{4,12},{12,4},... | collective-permute-start | bytes 393224 | tf_op jit(solution)/shard_map/ppermute | solution.py:27
  14.3 5.8 %collective-permute-start.2 = (bf16[128,512]{1,0:T(8,128)(2,1)S(1)}, bf16[128,512]{1,0:T(8,128)(2,1)S(1)}, u32[]{:S(2)}, u32[]{:S(2)}) collective-permute-start(bf16[128,512]{1,0:T(8,128)(2,1)S(1)} %collective-permute-done.1.refs_3_), channel_id=1, source_target_pairs={{0,1},{1,0},{2,3},{3,2},{4,5},{5,4},{6,7},{7,6},{8,9},{9,8},{10,11... | collective-permute-start | bytes 393224 | tf_op jit(solution)/shard_map/ppermute | solution.py:27
  17.1 9.4 %collective-permute-start.5 = (bf16[128,512]{1,0:T(8,128)(2,1)S(1)}, bf16[128,512]{1,0:T(8,128)(2,1)S(1)}, u32[]{:S(2)}, u32[]{:S(2)}) collective-permute-start(bf16[128,512]{1,0:T(8,128)(2,1)S(1)} %collective-permute-done.3.refs_5_), channel_id=1, source_target_pairs={{0,2},{2,0},{4,6},{6,4},{1,3},{3,1},{5,7},{7,5},{8,10},{10,8},{12,... | collective-permute-start | bytes 393224 | tf_op jit(solution)/shard_map/ppermute | solution.py:27
  18.7 7.9 %collective-permute-start.4 = (bf16[128,512]{1,0:T(8,128)(2,1)S(1)}, bf16[128,512]{1,0:T(8,128)(2,1)S(1)}, u32[]{:S(2)}, u32[]{:S(2)}) collective-permute-start(bf16[128,512]{1,0:T(8,128)(2,1)S(1)} %collective-permute-done.3.refs_5_), channel_id=1, source_target_pairs={{0,1},{1,0},{2,3},{3,2},{4,5},{5,4},{6,7},{7,6},{8,9},{9,8},{10,11... | collective-permute-start | bytes 393224 | tf_op jit(solution)/shard_map/ppermute | solution.py:27
  20.2 7.5 %collective-permute-start.6 = (bf16[128,512]{1,0:T(8,128)(2,1)S(1)}, bf16[128,512]{1,0:T(8,128)(2,1)S(1)}, u32[]{:S(2)}, u32[]{:S(2)}) collective-permute-start(bf16[128,512]{1,0:T(8,128)(2,1)S(1)} %collective-permute-done.2.refs_4_), channel_id=1, source_target_pairs={{0,4},{2,6},{4,0},{6,2},{1,5},{3,7},{5,1},{7,3},{8,12},{10,14},{12... | collective-permute-start | bytes 393224 | tf_op jit(solution)/shard_map/ppermute | solution.py:27
  28.9 5.7 %collective-permute-start.10 = (f32[16,72,128]{2,1,0:T(8,128)S(1)}, f32[16,72,128]{2,1,0:T(8,128)S(1)}, u32[]{:S(2)}, u32[]{:S(2)}) collective-permute-start(f32[16,72,128]{2,1,0:T(8,128)S(1)} %get-tuple-element.24), channel_id=1, source_target_pairs={{0,8},{8,0},{1,9},{9,1},{2,10},{10,2},{3,11},{11,3},{4,12},{12,4},... | collective-permute-start | bytes 1769480 | tf_op jit(solution)/shard_map/ppermute | solution.py:27

commit v5 on v4

--- a/solution.py
+++ b/solution.py
@@ -122,20 +122,19 @@
     early, found = early_slot(table, live, early_codes)
     total = live[0] * steps
     begin, end = (0, found * steps) if is_early else (found * steps, total)
-    index = begin + pl.program_id(0)
-    slot, step = slot_at(index // steps, early), index % steps
 
     def cubes_copy(at):
         side = at % 2
         source = block_of(blocks_ref, slot_at(at // steps, early), at % steps)
         return pltpu.make_async_copy(source, cubes_ref.at[side], sems.at[side])
 
-    @pl.when((index < end) & (index + 1 < total))
-    def _():
-        cubes_copy(index + 1).start()
-
-    @pl.when(index < end)
-    def _():
+    def multiply(index, carry):
+        slot, step = slot_at(index // steps, early), index % steps
+
+        @pl.when(index + 1 < total)
+        def _():
+            cubes_copy(index + 1).start()
+
         @pl.when(step == 0)
         def _():
             for code, ref in zip(codes, mode2_refs):
@@ -171,28 +170,29 @@
 
         pl.when(column % CORES == table[slot, 3])(functools.partial(add_to, kept_ref))
         pl.when(column % CORES != table[slot, 3])(functools.partial(add_to, sent_ref))
-
+        return carry
+
+    lax.fori_loop(begin, end, multiply, 0)
     if is_early:
 
-        @pl.when((index == end - 1) & (index + 1 < total))
+        @pl.when((end > begin) & (end < total))
         def _():
-            cubes_copy(index + 1).wait()
+            cubes_copy(end).wait()
 
         return
 
-    @pl.when(pl.program_id(0) == pl.num_programs(0) - 1)
-    def _():
-        for ref in (kept_ref, sent_ref):
-            bounds_at = ref.shape[1] - SUBLANES
-            most = jnp.abs(ref[:, :SUBLANES])
-            for row in range(SUBLANES, bounds_at, SUBLANES):
-                most = jnp.maximum(most, jnp.abs(ref[:, row : row + SUBLANES]))
-            ref[:, bounds_at:] = most
+    for ref in (kept_ref, sent_ref):
+        bounds_at = ref.shape[1] - SUBLANES
+        most = jnp.abs(ref[:, :SUBLANES])
+        for row in range(SUBLANES, bounds_at, SUBLANES):
+            most = jnp.maximum(most, jnp.abs(ref[:, row : row + SUBLANES]))
+        ref[:, bounds_at:] = most
 
 
 def products(early_codes, is_early, blocks, table, live_counts, pieces, mode3_pieces, buffers):
     slots, edge = blocks.shape[:2]
     codes = early_codes if is_early else tuple(range(len(pieces)))
+    in_smem = pl.BlockSpec(memory_space=pltpu.SMEM)
     panels = [pieces[code] for code in codes] + mode3_pieces
     rank = panels[0].shape[1]
     steps = edge // STEP_ROWS
@@ -205,17 +205,13 @@
     return pl.pallas_call(
         kernel,
         out_shape=[jax.ShapeDtypeStruct(buffer.shape, buffer.dtype) for buffer in buffers],
-        grid_spec=pltpu.PrefetchScalarGridSpec(
-            num_scalar_prefetch=2,
-            grid=(turns * steps,),
-            in_specs=[in_hbm] + [in_place] * (len(panels) + len(buffers)),
-            out_specs=[in_place] * len(buffers),
-            scratch_shapes=[
-                pltpu.VMEM((edge, rank), jnp.float32),
-                pltpu.VMEM((edge, rank), mode3_pieces[0].dtype),
-                pltpu.SemaphoreType.DMA((2,)),
-            ],
-        ),
+        in_specs=[in_smem] * 2 + [in_hbm] + [in_place] * (len(panels) + len(buffers)),
+        out_specs=[in_place] * len(buffers),
+        scratch_shapes=[
+            pltpu.VMEM((edge, rank), jnp.float32),
+            pltpu.VMEM((edge, rank), mode3_pieces[0].dtype),
+            pltpu.SemaphoreType.DMA((2,)),
+        ],
         cost_estimate=pl.CostEstimate(
             flops=2 * turns * edge**3 * rank,
             bytes_accessed=2 * turns * edge**3,

time: 60.8 us -> 60.4 us (level)
  no operation moved by 1% of the time
where the time goes in v5:
time: 60.4 us; the launch traced here: 60.1 us
  blocking collectives  25.2 us (42%)
  starting transfers between devices  17 us (28%)
  Pallas kernels  9.31 us (15%)
  waiting for transfers between devices  6.8 us (11%)
  other arithmetic  1.03 us (2%)
  between operations  0.74 us (1%)
    all_to_all x1, blocking collectives, on_device(): lax.all_to_all(packed, CHIPS, 0, 0, tiled=True).astype(jnp.float32)  25.2 us
    ppermute x11, starting transfers between devices, exchange(): return lax.ppermute(value, axis, [(i, i ^ code) for i in range(size)])  17 us
    ppermute x11, waiting for transfers between devices, exchange(): return lax.ppermute(value, axis, [(i, i ^ code) for i in range(size)])  6.8 us
    pallas_call x2, Pallas kernels, products(): pl.pallas_call(kernel, out_shape=[jax.ShapeDtypeStruct(buffer.shape, buff...  6.36 us
    pallas_call x1, Pallas kernels, fetch_local(): pl.pallas_call(functools.partial(fetch_kernel, early_codes), out_shape=[j...  2.21 us
  transfers between devices with their start and end apart: 11, of which 3 were waited for; matrix products, arithmetic and copies ran while one was open for 2% of the time, Pallas kernels for 13%

profile of v5, /device:TPU:0, one launch (start us, length us, event | category | flops | bytes accessed | tf_op | source)
XLA Modules:
  0.0 60.1 jit_solution(8704146939890313899)
XLA Ops:
  0.0 3.0 %collective-permute-start.8 = (bf16[128,512]{1,0:T(8,128)(2,1)}, bf16[128,512]{1,0:T(8,128)(2,1)S(1)}, u32[]{:S(2)}, u32[]{:S(2)}) collective-permute-start(bf16[128,512]{1,0:T(8,128)(2,1)} %mode3_ref.1), channel_id=1, source_target_pairs={{0,16},{16,0},{1,17},{17,1},{2,18},{18,2},{3,19},{19,3},{4,20},{20... | collective-permute-start | bytes 393224 | tf_op jit(solution)/shard_map/ppermute | solution.py:27
  3.0 0.0 collective-permute-start.7
  3.0 1.5 %collective-permute-start = (bf16[128,512]{1,0:T(8,128)(2,1)}, bf16[128,512]{1,0:T(8,128)(2,1)S(1)}, u32[]{:S(2)}, u32[]{:S(2)}) collective-permute-start(bf16[128,512]{1,0:T(8,128)(2,1)} %mode2_ref.1), channel_id=1, source_target_pairs={{0,1},{1,0},{2,3},{3,2},{4,5},{5,4},{6,7},{7,6},{8,9},{9,8},{10,11... | collective-permute-start | bytes 393224 | tf_op jit(solution)/shard_map/ppermute | solution.py:27
  4.5 2.6 %collective-permute-start.3 = (bf16[128,512]{1,0:T(8,128)(2,1)}, bf16[128,512]{1,0:T(8,128)(2,1)S(1)}, u32[]{:S(2)}, u32[]{:S(2)}) collective-permute-start(bf16[128,512]{1,0:T(8,128)(2,1)} %mode2_ref.1), channel_id=1, source_target_pairs={{0,4},{2,6},{4,0},{6,2},{1,5},{3,7},{5,1},{7,3},{8,12},{10,14},{12... | collective-permute-start | bytes 393224 | tf_op jit(solution)/shard_map/ppermute | solution.py:27
  7.1 1.6 %collective-permute-start.1 = (bf16[128,512]{1,0:T(8,128)(2,1)}, bf16[128,512]{1,0:T(8,128)(2,1)S(1)}, u32[]{:S(2)}, u32[]{:S(2)}) collective-permute-start(bf16[128,512]{1,0:T(8,128)(2,1)} %mode2_ref.1), channel_id=1, source_target_pairs={{0,2},{2,0},{4,6},{6,4},{1,3},{3,1},{5,7},{7,5},{8,10},{10,8},{12,... | collective-permute-start | bytes 393224 | tf_op jit(solution)/shard_map/ppermute | solution.py:27
  9.3 0.1 pad.3.clone
  9.4 0.9 %fusion.4 = (s32[4,1]{1,0:T(4,128)S(1)}, s32[4,1]{1,0:T(4,128)S(1)}, s32[4,1]{1,0:T(4,128)S(1)}) fusion(s32[4,3]{1,0:T(4,128)} %param.6, s32[]{:T(128)S(6)} %add.7, s32[]{:T(128)S(6)} %add.6), kind=kLoop, calls=%fused_computation.9 | loop fusion | flops 56 | bytes 104 | tf_op jit(solution)/shard_map/slice | solution.py:258
  10.3 0.0 collective-permute-done.8.refs_8_.refs_11_
  10.3 0.1 collective-permute-start.9
  10.3 4.0 %collective-permute-done.1.refs_3_ = bf16[128,512]{1,0:T(8,128)(2,1)S(1)} collective-permute-done((bf16[128,512]{1,0:T(8,128)(2,1)}, bf16[128,512]{1,0:T(8,128)(2,1)S(1)}, u32[]{:S(2)}, u32[]{:S(2)}) %collective-permute-start.1) | collective-permute-done | bytes 131104 | tf_op jit(solution)/shard_map/ppermute | solution.py:27
  14.3 0.5 collective-permute-start.2
  14.8 0.1 add_add_fusion.table
  14.9 2.2 %shard_map.55 = (bf16[2,64,128,128]{3,2,1,0:T(8,128)(2,1)S(1)}, bf16[128,512]{1,0:T(8,128)(2,1)S(1)}, bf16[128,512]{1,0:T(8,128)(2,1)S(1)}, f32[16,72,128]{2,1,0:T(8,128)S(1)}, f32[16,72,128]{2,1,0:T(8,128)S(1)}) custom-call(s32[4,4]{1,0:T(4,128)S(1)} %add_add_fusion.table, s32[1]{0:T(128)S(6)} %copy.18.live, bf16[4,128,128,128]{3,2,1,0:T(8,128)(2,1)} %refs_0_.3, ...), custom_call_target="tpu_custom_call" | custom-call | bytes 4194304 | tf_op jit(solution)/shard_map/pallas_call | solution.py:100
  17.1 0.0 collective-permute-done.3.refs_5_
  17.1 1.5 %collective-permute-start.5 = (bf16[128,512]{1,0:T(8,128)(2,1)S(1)}, bf16[128,512]{1,0:T(8,128)(2,1)S(1)}, u32[]{:S(2)}, u32[]{:S(2)}) collective-permute-start(bf16[128,512]{1,0:T(8,128)(2,1)S(1)} %collective-permute-done.3.refs_5_), channel_id=1, source_target_pairs={{0,2},{2,0},{4,6},{6,4},{1,3},{3,1},{5,7},{7,5},{8,10},{10,8},{12,... | collective-permute-start | bytes 393224 | tf_op jit(solution)/shard_map/ppermute | solution.py:27
  18.6 0.0 collective-permute-done.7.refs_7_.refs_10_
  18.7 1.5 %collective-permute-start.4 = (bf16[128,512]{1,0:T(8,128)(2,1)S(1)}, bf16[128,512]{1,0:T(8,128)(2,1)S(1)}, u32[]{:S(2)}, u32[]{:S(2)}) collective-permute-start(bf16[128,512]{1,0:T(8,128)(2,1)S(1)} %collective-permute-done.3.refs_5_), channel_id=1, source_target_pairs={{0,1},{1,0},{2,3},{3,2},{4,5},{5,4},{6,7},{7,6},{8,9},{9,8},{10,11... | collective-permute-start | bytes 393224 | tf_op jit(solution)/shard_map/ppermute | solution.py:27
  20.2 0.0 collective-permute-done.2.refs_4_
  20.2 0.7 %collective-permute-start.6 = (bf16[128,512]{1,0:T(8,128)(2,1)S(1)}, bf16[128,512]{1,0:T(8,128)(2,1)S(1)}, u32[]{:S(2)}, u32[]{:S(2)}) collective-permute-start(bf16[128,512]{1,0:T(8,128)(2,1)S(1)} %collective-permute-done.2.refs_4_), channel_id=1, source_target_pairs={{0,4},{2,6},{4,0},{6,2},{1,5},{3,7},{5,1},{7,3},{8,12},{10,14},{12... | collective-permute-start | bytes 393224 | tf_op jit(solution)/shard_map/ppermute | solution.py:27
  20.8 0.0 collective-permute-done.refs_2_
  20.8 0.0 collective-permute-done.9.refs_9_.refs_12_
  20.8 5.7 %shard_map.56 = (bf16[2,64,128,128]{3,2,1,0:T(8,128)(2,1)S(1)}, f32[16,72,128]{2,1,0:T(8,128)S(1)}, f32[16,72,128]{2,1,0:T(8,128)S(1)}) custom-call(s32[4,4]{1,0:T(4,128)S(1)} %add_add_fusion.table, s32[1]{0:T(128)S(6)} %copy.18.live, bf16[4,128,128,128]{3,2,1,0:T(8,128)(2,1)} %refs_0_.3, ...), custom_call_target="tpu_custom_call", output_to_operand_aliasing={{0}: (12, {}), {1}: (13, {}), {2}: (14, {})} | custom-call | flops 2147483648 | bytes 4194304 | tf_op jit(solution)/shard_map/pallas_call | solution.py:205
  26.5 0.0 collective-permute-done.5.refs_7_
  26.5 0.0 collective-permute-done.4.refs_6_
  26.6 1.2 %collective-permute-done.6.refs_8_ = bf16[128,512]{1,0:T(8,128)(2,1)S(1)} collective-permute-done((bf16[128,512]{1,0:T(8,128)(2,1)S(1)}, bf16[128,512]{1,0:T(8,128)(2,1)S(1)}, u32[]{:S(2)}, u32[]{:S(2)}) %collective-permute-start.6) | collective-permute-done | bytes 131104 | tf_op jit(solution)/shard_map/ppermute | solution.py:27
  27.7 0.7 %shard_map.57 = (bf16[2,64,128,128]{3,2,1,0:T(8,128)(2,1)S(1)}, f32[16,72,128]{2,1,0:T(8,128)S(1)}, f32[16,72,128]{2,1,0:T(8,128)S(1)}) custom-call(s32[4,4]{1,0:T(4,128)S(1)} %add_add_fusion.table, s32[1]{0:T(128)S(6)} %copy.18.live, bf16[4,128,128,128]{3,2,1,0:T(8,128)(2,1)} %refs_0_.3, ...), custom_call_target="tpu_custom_call", output_to_operand_aliasing={{0}: (15, {}), {1}: (16, {}), {2}: (17, {})} | custom-call | flops 8589934592 | bytes 16777216 | tf_op jit(solution)/shard_map/pallas_call | solution.py:205
  28.4 4.1 %collective-permute-start.10 = (f32[16,72,128]{2,1,0:T(8,128)S(1)}, f32[16,72,128]{2,1,0:T(8,128)S(1)}, u32[]{:S(2)}, u32[]{:S(2)}) collective-permute-start(f32[16,72,128]{2,1,0:T(8,128)S(1)} %get-tuple-element.24), channel_id=1, source_target_pairs={{0,8},{8,0},{1,9},{9,1},{2,10},{10,2},{3,11},{11,3},{4,12},{12,4},... | collective-permute-start | bytes 1769480 | tf_op jit(solution)/shard_map/ppermute | solution.py:27
  32.5 1.6 %collective-permute-done.10.received_ref = f32[16,72,128]{2,1,0:T(8,128)S(1)} collective-permute-done((f32[16,72,128]{2,1,0:T(8,128)S(1)}, f32[16,72,128]{2,1,0:T(8,128)S(1)}, u32[]{:S(2)}, u32[]{:S(2)}) %collective-permute-start.10) | collective-permute-done | bytes 589856 | tf_op jit(solution)/shard_map/ppermute | solution.py:27
  34.1 0.1 shard_map.58
  34.3 25.2 %all_to_all.5 = f16[16,72,128]{2,1,0:T(8,128)(2,1)S(1)} all-to-all(f16[16,72,128]{2,1,0:T(8,128)(2,1)S(1)} %convert_element_type.6), channel_id=1, replica_groups=mesh['x'=2,'core'=2,'z'=4,'y'=2] {'x','z','y'}, dimensions={0} | all-to-all | bytes 589824 | tf_op jit(solution)/shard_map/all_to_all | solution.py:287
  59.5 0.7 %shard_map.59 = f32[16,512]{1,0:T(8,128)} custom-call(f32[16,72,128]{2,1,0:T(8,128)S(1)} %convert_element_type.7.arrived_ref), custom_call_target="tpu_custom_call" | custom-call | tf_op jit(solution)/shard_map/pallas_call | solution.py:288
  (2 shorter events, 0.1 us)
Async XLA Ops:
  0.0 10.3 %collective-permute-start.8 = (bf16[128,512]{1,0:T(8,128)(2,1)}, bf16[128,512]{1,0:T(8,128)(2,1)S(1)}, u32[]{:S(2)}, u32[]{:S(2)}) collective-permute-start(bf16[128,512]{1,0:T(8,128)(2,1)} %mode3_ref.1), channel_id=1, source_target_pairs={{0,16},{16,0},{1,17},{17,1},{2,18},{18,2},{3,19},{19,3},{4,20},{20... | collective-permute-start | bytes 393224 | tf_op jit(solution)/shard_map/ppermute | solution.py:27
  3.0 15.7 %collective-permute-start.7 = (bf16[128,512]{1,0:T(8,128)(2,1)}, bf16[128,512]{1,0:T(8,128)(2,1)S(1)}, u32[]{:S(2)}, u32[]{:S(2)}) collective-permute-start(bf16[128,512]{1,0:T(8,128)(2,1)} %mode3_ref.1), channel_id=1, source_target_pairs={{0,8},{8,0},{1,9},{9,1},{2,10},{10,2},{3,11},{11,3},{4,12},{12,4},... | collective-permute-start | bytes 393224 | tf_op jit(solution)/shard_map/ppermute | solution.py:27
  3.0 17.9 %collective-permute-start = (bf16[128,512]{1,0:T(8,128)(2,1)}, bf16[128,512]{1,0:T(8,128)(2,1)S(1)}, u32[]{:S(2)}, u32[]{:S(2)}) collective-permute-start(bf16[128,512]{1,0:T(8,128)(2,1)} %mode2_ref.1), channel_id=1, source_target_pairs={{0,1},{1,0},{2,3},{3,2},{4,5},{5,4},{6,7},{7,6},{8,9},{9,8},{10,11... | collective-permute-start | bytes 393224 | tf_op jit(solution)/shard_map/ppermute | solution.py:27
  4.5 12.6 %collective-permute-start.3 = (bf16[128,512]{1,0:T(8,128)(2,1)}, bf16[128,512]{1,0:T(8,128)(2,1)S(1)}, u32[]{:S(2)}, u32[]{:S(2)}) collective-permute-start(bf16[128,512]{1,0:T(8,128)(2,1)} %mode2_ref.1), channel_id=1, source_target_pairs={{0,4},{2,6},{4,0},{6,2},{1,5},{3,7},{5,1},{7,3},{8,12},{10,14},{12... | collective-permute-start | bytes 393224 | tf_op jit(solution)/shard_map/ppermute | solution.py:27
  7.1 7.3 %collective-permute-start.1 = (bf16[128,512]{1,0:T(8,128)(2,1)}, bf16[128,512]{1,0:T(8,128)(2,1)S(1)}, u32[]{:S(2)}, u32[]{:S(2)}) collective-permute-start(bf16[128,512]{1,0:T(8,128)(2,1)} %mode2_ref.1), channel_id=1, source_target_pairs={{0,2},{2,0},{4,6},{6,4},{1,3},{3,1},{5,7},{7,5},{8,10},{10,8},{12,... | collective-permute-start | bytes 393224 | tf_op jit(solution)/shard_map/ppermute | solution.py:27
  10.3 10.6 %collective-permute-start.9 = (bf16[128,512]{1,0:T(8,128)(2,1)S(1)}, bf16[128,512]{1,0:T(8,128)(2,1)S(1)}, u32[]{:S(2)}, u32[]{:S(2)}) collective-permute-start(bf16[128,512]{1,0:T(8,128)(2,1)S(1)} %collective-permute-done.8.refs_8_.refs_11_), channel_id=1, source_target_pairs={{0,8},{8,0},{1,9},{9,1},{2,10},{10,2},{3,11},{11,3},{4,12},{12,4},... | collective-permute-start | bytes 393224 | tf_op jit(solution)/shard_map/ppermute | solution.py:27
  14.3 5.8 %collective-permute-start.2 = (bf16[128,512]{1,0:T(8,128)(2,1)S(1)}, bf16[128,512]{1,0:T(8,128)(2,1)S(1)}, u32[]{:S(2)}, u32[]{:S(2)}) collective-permute-start(bf16[128,512]{1,0:T(8,128)(2,1)S(1)} %collective-permute-done.1.refs_3_), channel_id=1, source_target_pairs={{0,1},{1,0},{2,3},{3,2},{4,5},{5,4},{6,7},{7,6},{8,9},{9,8},{10,11... | collective-permute-start | bytes 393224 | tf_op jit(solution)/shard_map/ppermute | solution.py:27
  17.1 9.4 %collective-permute-start.5 = (bf16[128,512]{1,0:T(8,128)(2,1)S(1)}, bf16[128,512]{1,0:T(8,128)(2,1)S(1)}, u32[]{:S(2)}, u32[]{:S(2)}) collective-permute-start(bf16[128,512]{1,0:T(8,128)(2,1)S(1)} %collective-permute-done.3.refs_5_), channel_id=1, source_target_pairs={{0,2},{2,0},{4,6},{6,4},{1,3},{3,1},{5,7},{7,5},{8,10},{10,8},{12,... | collective-permute-start | bytes 393224 | tf_op jit(solution)/shard_map/ppermute | solution.py:27
  18.7 7.9 %collective-permute-start.4 = (bf16[128,512]{1,0:T(8,128)(2,1)S(1)}, bf16[128,512]{1,0:T(8,128)(2,1)S(1)}, u32[]{:S(2)}, u32[]{:S(2)}) collective-permute-start(bf16[128,512]{1,0:T(8,128)(2,1)S(1)} %collective-permute-done.3.refs_5_), channel_id=1, source_target_pairs={{0,1},{1,0},{2,3},{3,2},{4,5},{5,4},{6,7},{7,6},{8,9},{9,8},{10,11... | collective-permute-start | bytes 393224 | tf_op jit(solution)/shard_map/ppermute | solution.py:27
  20.2 7.5 %collective-permute-start.6 = (bf16[128,512]{1,0:T(8,128)(2,1)S(1)}, bf16[128,512]{1,0:T(8,128)(2,1)S(1)}, u32[]{:S(2)}, u32[]{:S(2)}) collective-permute-start(bf16[128,512]{1,0:T(8,128)(2,1)S(1)} %collective-permute-done.2.refs_4_), channel_id=1, source_target_pairs={{0,4},{2,6},{4,0},{6,2},{1,5},{3,7},{5,1},{7,3},{8,12},{10,14},{12... | collective-permute-start | bytes 393224 | tf_op jit(solution)/shard_map/ppermute | solution.py:27
  28.4 5.7 %collective-permute-start.10 = (f32[16,72,128]{2,1,0:T(8,128)S(1)}, f32[16,72,128]{2,1,0:T(8,128)S(1)}, u32[]{:S(2)}, u32[]{:S(2)}) collective-permute-start(f32[16,72,128]{2,1,0:T(8,128)S(1)} %get-tuple-element.24), channel_id=1, source_target_pairs={{0,8},{8,0},{1,9},{9,1},{2,10},{10,2},{3,11},{11,3},{4,12},{12,4},... | collective-permute-start | bytes 1769480 | tf_op jit(solution)/shard_map/ppermute | solution.py:27
